TPU v7x, 128 devices: a whole 4x4x4 slice. The times are simulated.
128 devices in a mesh: ctx: 16 (over z, y), head: 8 (over x, core).
Axes of the slice: x: 4, y: 4, z: 4, core: 2. Of those that a mesh axis runs over, the one named last changes fastest.
Arguments:
- queries: bfloat16 [8192, 8192], P('ctx', 'head'), may hold values from -6 to 6
- keys: bfloat16 [8192, 8192], P('ctx', 'head'), may hold values from -6 to 6
- values: bfloat16 [8192, 8192], P('ctx', 'head'), may hold values from -6 to 6
- teacher: bfloat16 [8192, 5120], P('ctx', 'head'), may hold values from -6 to 6
- out_weight: bfloat16 [8192, 5120], P('head'), may hold values from -0.0625 to 0.0625
- valid: int32 [8192], P('ctx'), may hold values from 0 to 1, as said below
Outputs:
- q_grad: float32 [8192, 8192], P('ctx', 'head')
- k_grad: float32 [8192, 8192], P('ctx', 'head')
- v_grad: float32 [8192, 8192], P('ctx', 'head')
Inputs may be any that keep to these rules, and one draw needn't show every extreme that they name: The last token always has valid = 1.
All inputs are finite; a program needn't handle non-finite values.
Results may differ from a plain program's by a relative error of at most 0.012.
Values may be sent and summed in bfloat16 or wider, within the bound.
A program may use at most 128 MiB of HBM per device.

v0:
```python
import math

import jax
import jax.numpy as jnp
from jax import lax
from jax.sharding import PartitionSpec as P

DH = 128


def entering(x, axis, join, neutral, backward):
    count = lax.axis_size(axis)
    place = lax.axis_index(axis)
    ahead = count - 1 - place if backward else place
    gathered = lax.all_gather(x.astype(jnp.bfloat16), axis)
    state = jnp.zeros_like(x) + jnp.asarray(neutral, x.dtype)

    def one(turn, state):
        source = count - 1 - turn if backward else turn
        return join(state, lax.dynamic_index_in_dim(gathered, source, 0, False).astype(x.dtype))

    return lax.fori_loop(0, ahead, one, state)


def add_states(earlier, later):
    return earlier + later


def on_device(queries, keys, values, teacher, out_weight, valid):
    precise = lax.Precision.HIGHEST
    tok_rows, col_width = queries.shape
    head_count = col_width // DH
    ctx_size = lax.axis_size("ctx")
    attn_scale = 1.0 / math.sqrt(DH * tok_rows * ctx_size)
    blk_rows = math.gcd(tok_rows, 512)
    blk_count = tok_rows // blk_rows
    causal = jnp.tril(jnp.ones((blk_rows, blk_rows), jnp.float32))
    query_b = queries.reshape(blk_count, blk_rows, head_count, DH)
    key_b = keys.reshape(blk_count, blk_rows, head_count, DH)
    value_b = values.reshape(blk_count, blk_rows, head_count, DH)
    query_f = query_b.astype(jnp.float32)
    key_f = key_b.astype(jnp.float32)
    value_f = value_b.astype(jnp.float32)
    block_kv = jnp.einsum("nthd,nthe->nhde", key_b, value_b, preferred_element_type=jnp.float32)
    kv_local = jnp.sum(block_kv, 0)
    count_local = jnp.sum(valid).astype(jnp.float32)
    kv_prefix = entering(kv_local, "ctx", add_states, jnp.zeros_like(kv_local), False)
    valid_total = lax.psum(count_local, "ctx")
    starts = kv_prefix[None] + (jnp.cumsum(block_kv, 0) - block_kv)
    scores = (
        jnp.einsum("nthd,nshd->nhts", query_b, key_b, preferred_element_type=jnp.float32) * causal
    )
    outputs = jnp.einsum("nhts,nshe->nthe", scores, value_f, precision=precise)
    outputs = outputs + jnp.einsum("nthd,nhde->nthe", query_f, starts, precision=precise)
    attn = (attn_scale * outputs).reshape(tok_rows, col_width).astype(jnp.bfloat16)
    terms = jnp.dot(attn, out_weight, preferred_element_type=jnp.float32)
    predicted = lax.psum_scatter(
        terms.astype(jnp.bfloat16), "head", scatter_dimension=1, tiled=True
    ).astype(jnp.float32)
    residual_err = predicted - teacher.astype(jnp.float32)
    factor = tok_rows * ctx_size / valid_total
    error_grad = (valid.astype(jnp.float32)[:, None] * residual_err * factor).astype(jnp.bfloat16)
    attn_grad = lax.dot_general(
        lax.all_gather(error_grad, "head", axis=1, tiled=True),
        out_weight,
        (((1,), (1,)), ((), ())),
        preferred_element_type=jnp.float32,
    )
    grad_f = attn_grad.reshape(blk_count, blk_rows, head_count, DH)
    block_r = jnp.einsum("nthd,nthe->nhde", query_f, grad_f, precision=precise)
    r_local = jnp.sum(block_r, 0)
    r_after = entering(r_local, "ctx", add_states, jnp.zeros_like(r_local), True)
    later = r_after[None] + (r_local[None] - jnp.cumsum(block_r, 0))
    grad_scores = jnp.einsum("nthe,nshe->nhts", grad_f, value_f, precision=precise) * causal
    q_grad = jnp.einsum("nhts,nshd->nthd", grad_scores, key_f, precision=precise)
    q_grad = q_grad + jnp.einsum("nhde,nthe->nthd", starts, grad_f, precision=precise)
    k_grad = jnp.einsum("nhts,nthd->nshd", grad_scores, query_f, precision=precise)
    k_grad = k_grad + jnp.einsum("nhde,nshe->nshd", later, value_f, precision=precise)
    v_grad = jnp.einsum("nhts,nthe->nshe", scores, grad_f, precision=precise)
    v_grad = v_grad + jnp.einsum("nhde,nshd->nshe", later, key_f, precision=precise)
    return (
        (attn_scale * q_grad).reshape(tok_rows, col_width),
        (attn_scale * k_grad).reshape(tok_rows, col_width),
        (attn_scale * v_grad).reshape(tok_rows, col_width),
    )


def solution(mesh):
    in_specs = (
        P("ctx", "head"),
        P("ctx", "head"),
        P("ctx", "head"),
        P("ctx", "head"),
        P("head", None),
        P("ctx"),
    )
    out_specs = (P("ctx", "head"), P("ctx", "head"), P("ctx", "head"))
    return jax.shard_map(
        on_device, mesh=mesh, in_specs=in_specs, out_specs=out_specs, check_vma=False
    )
```

profile of v0, /device:TPU:1, one launch (start us, length us, event | category | flops | bytes accessed | tf_op | source)
XLA Modules:
  0.0 306.1 jit_solution(6113395252601902396)
XLA Ops:
  7.2 0.0 copy-start
  7.2 0.0 all-gather.8.cloned.1.call-start
  7.2 1.6 copy.62
  8.8 0.7 copy.35
  9.5 0.0 copy-start.5
  9.5 1.3 fusion.49
  10.9 0.0 all-gather.8.cloned.1.call-update
  10.9 0.0 reduce-scatter.4.cloned.1.call-start
  10.9 0.1 fusion.36
  11.1 0.3 copy-done.5
  11.4 5.7 %fusion.28 = f32[8,512,512]{2,1,0:T(8,128)} fusion(bf16[512,1024]{1,0:T(8,128)(2,1)} %param.11, bf16[512,1024]{1,0:T(8,128)(2,1)S(1)} %copy-done.5), kind=kOutput, calls=%fused_computation.32 | convolution fusion | flops 536870912 | bytes 10485760 | tf_op jit(solution)/shard_map/nthd,nshd->nhts/dot_general | solution.py:51
  17.1 48.4 %all-gather.8.cloned.1.call-done = bf16[128,128,128]{2,1,0:T(8,128)(2,1)} async-done(((bf16[8,128,128]{2,1,0:T(8,128)(2,1)}), bf16[128,128,128]{2,1,0:T(8,128)(2,1)}) %all-gather.8.cloned.1.call-update) | async-done | bytes 4194320 | tf_op jit(solution)/shard_map/all_gather | solution.py:15
  65.6 0.0 copy-start.14
  65.7 1.0 copy-done.14
  66.7 2.3 fusion.34
  68.9 8.6 %fusion.16 = bf16[8,128,512]{2,1,0:T(8,128)(2,1)S(1)} fusion(f32[8,128,512]{2,1,0:T(8,128)S(1)} %fusion.34, f32[8,512,512]{2,1,0:T(8,128)} %fusion.28, f32[512,512]{1,0:T(8,128)S(1)} %fusion.36, bf16[512,1024]{1,0:T(8,128)(2,1)S(1)} %copy-done), kind=kOutput, calls=%fused_computation.23 | convolution fusion | flops 3224895488 | bytes 13631488 | tf_op jit(solution)/shard_map/nhts,nshe->nthe/dot_general | solution.py:53
  77.5 11.4 %convolution_convert_fusion = bf16[512,5120]{1,0:T(8,128)(2,1)} fusion(bf16[512,1024]{0,1:T(8,128)(2,1)S(1)} %bitcast.153, bf16[1024,5120]{1,0:T(8,128)(2,1)} %param.14), kind=kOutput, calls=%fused_computation.10 | convolution fusion | flops 5371330560 | bytes 16777216 | tf_op jit(solution)/shard_map/dot_general | solution.py:56
  88.9 7.8 %copy.57 = bf16[512,5120]{0,1:T(8,128)(2,1)} copy(bf16[512,5120]{1,0:T(8,128)(2,1)} %convolution_convert_fusion) | data formatting | bytes 10485760
  96.7 0.0 reduce-scatter.4.cloned.1.call-update
  96.7 0.0 all-gather.6.cloned.1.call-start
  96.8 0.6 copy-done.15
  97.4 0.6 fusion.48
  98.6 57.7 %psum.7 = f32[]{:T(128)} all-reduce(f32[]{:T(128)S(6)} %convert_element_type.75), channel_id=1, replica_groups=mesh['ctx'=16,'head'=8] {'ctx'}, use_global_device_ids=true, to_apply=%region_4.5 | all-reduce | flops 1 | bytes 8 | tf_op jit(solution)/shard_map/psum | solution.py:48
  157.0 0.0 reduce-scatter.4.cloned.1.call-done
  157.0 2.2 copy.58
  159.2 2.4 multiply_convert_fusion
  161.6 0.0 all-gather.6.cloned.1.call-update
  161.6 0.0 all-gather.10.cloned.1.call-start
  161.6 40.5 %all-gather.6.cloned.1.call-done = bf16[512,5120]{1,0:T(8,128)(2,1)} async-done(((bf16[512,640]{1,0:T(8,128)(2,1)}), bf16[512,5120]{1,0:T(8,128)(2,1)}) %all-gather.6.cloned.1.call-update) | async-done | bytes 5242896 | tf_op jit(solution)/shard_map/all_gather | solution.py:64
  202.1 10.0 %fusion.50 = f32[512,1024]{0,1:T(8,128)S(1)} fusion(bf16[512,5120]{1,0:T(8,128)(2,1)} %all-gather.6.cloned.1.call-done, bf16[1024,5120]{1,0:T(8,128)(2,1)} %param.14), kind=kOutput, calls=%fused_computation.58 | convolution fusion | flops 5368709120 | bytes 17825792 | tf_op jit(solution)/shard_map/dot_general | solution.py:63
  212.1 0.0 copy-start.2
  212.1 1.3 copy-done.2
  213.4 1.2 fusion.31
  214.7 0.8 copy-done.11
  215.5 0.8 copy.46
  216.4 0.0 all-gather.10.cloned.1.call-update
  216.4 3.7 %fusion.47 = f32[8,512,128]{1,2,0:T(8,128)S(1)} fusion(f32[512,8,128]{0,2,1:T(8,128)} %bitcast.144, f32[8,128,128]{2,1,0:T(8,128)S(1)} %get-tuple-element.82, f32[8,128,128]{2,1,0:T(8,128)S(1)} %copy-done.14), kind=kOutput, calls=%fused_computation.55 | convolution fusion | flops 805568512 | bytes 5242880 | tf_op jit(solution)/shard_map/nhde,nthe->nthd/dot_general | solution.py:76
  220.1 3.5 %fusion.23 = f32[8,512,512]{2,1,0:T(8,128)S(1)} fusion(f32[512,8,128]{0,2,1:T(8,128)S(1)} %bitcast.145, bf16[512,1024]{1,0:T(8,128)(2,1)S(1)} %copy-done), kind=kOutput, calls=%fused_computation.27 | convolution fusion | flops 3221225472 | bytes 11534336 | tf_op jit(solution)/shard_map/nthe,nshe->nhts/dot_general | solution.py:74
  223.7 6.6 %fusion.14 = f32[1,512,8,128]{1,3,2,0:T(8,128)} fusion(f32[8,512,128]{1,2,0:T(8,128)S(1)} %fusion.47, bf16[512,8,128]{0,2,1:T(8,128)(2,1)S(1)} %copy-done.9, f32[8,512,512]{2,1,0:T(8,128)S(1)} %fusion.23, f32[512,512]{1,0:T(8,128)S(1)} %fusion.36), kind=kOutput, calls=%fused_computation.20 | convolution fusion | flops 3224371200 | bytes 14680064 | tf_op jit(solution)/shard_map/nhts,nshd->nthd/dot_general | solution.py:75
  230.3 3.0 copy.52
  233.3 8.4 %fusion = f32[8,512,128]{1,2,0:T(8,128)} fusion(f32[8,512,512]{2,1,0:T(8,128)} %copy-done.1, f32[512,512]{1,0:T(8,128)S(1)} %fusion.36, bf16[512,1024]{1,0:T(8,128)(2,1)S(1)} %copy-done.7), kind=kOutput, calls=%fused_computation.2 | convolution fusion | flops 3223322624 | bytes 12582912 | tf_op jit(solution)/shard_map/nhts,nthd->nshd/dot_general | solution.py:77
  241.7 8.9 %fusion.4 = f32[8,128,512]{2,1,0:T(8,128)} fusion(f32[512,8,128]{0,2,1:T(8,128)S(1)} %bitcast.146, f32[8,512,512]{2,1,0:T(8,128)} %fusion.28, f32[512,512]{1,0:T(8,128)S(1)} %fusion.36), kind=kOutput, calls=%fused_computation.6 | convolution fusion | flops 3223322624 | bytes 13631488 | tf_op jit(solution)/shard_map/nhts,nthe->nshe/dot_general | solution.py:79
  250.6 17.0 %all-gather.10.cloned.1.call-done = bf16[128,128,128]{2,1,0:T(8,128)(2,1)} async-done(((bf16[8,128,128]{2,1,0:T(8,128)(2,1)}), bf16[128,128,128]{2,1,0:T(8,128)(2,1)}) %all-gather.10.cloned.1.call-update) | async-done | bytes 4194320 | tf_op jit(solution)/shard_map/all_gather | solution.py:15
  267.6 16.6 %while.23 = (s32[]{:T(128)}, f32[8,128,128]{2,1,0:T(8,128)S(1)}, s32[]{:T(128)}, bf16[16,8,128,128]{3,2,1,0:T(8,128)(2,1)}, s32[]{:T(128)}, /*index=5*/s32[]{:T(128)}, s32[]{:T(128)}, s32[]{:T(128)}) while((s32[]{:T(128)}, f32[8,128,128]{2,1,0:T(8,128)S(1)}, s32[]{:T(128)}, bf16[16,8,128,128]{3,2,1,0:T(8,128)(2,1)}, s32[]{:T(128)}, ...), condition=%wide.region_6.7_spmd, body=%wide.region_5.6_spmd.sunk | while | flops 262150 | bytes 1310855 | solution.py:22
  267.6 1.2 convert_add_fusion.5
  268.8 1.1 convert_add_fusion.5
  269.9 1.1 convert_add_fusion.5
  271.0 1.1 convert_add_fusion.5
  272.1 1.1 convert_add_fusion.5
  273.2 1.1 convert_add_fusion.5
  274.3 1.1 convert_add_fusion.5
  275.4 1.1 convert_add_fusion.5
  276.5 1.1 convert_add_fusion.5
  277.6 1.1 convert_add_fusion.5
  278.7 1.1 convert_add_fusion.5
  279.8 1.1 convert_add_fusion.5
  280.9 1.1 convert_add_fusion.5
  282.0 1.1 convert_add_fusion.5
  283.1 1.1 convert_add_fusion.5
  284.2 1.0 copy.47
  285.2 4.2 %fusion.12 = f32[1,512,8,128]{1,3,2,0:T(8,128)} fusion(f32[8,128,512]{2,1,0:T(8,128)} %fusion.4, f32[8,128,128]{1,2,0:T(8,128)} %copy.47, f32[8,128,128]{2,1,0:T(8,128)S(1)} %copy-done.12, bf16[512,1024]{1,0:T(8,128)(2,1)S(1)} %copy-done.10), kind=kOutput, calls=%fused_computation.16 | convolution fusion | flops 806617088 | bytes 6291456 | tf_op jit(solution)/shard_map/nhde,nshd->nshe/dot_general | solution.py:80
  289.3 2.9 copy.54
  292.3 4.0 %fusion.13 = f32[1,512,8,128]{1,3,2,0:T(8,128)} fusion(f32[8,512,128]{1,2,0:T(8,128)} %fusion, f32[8,128,128]{1,2,0:T(8,128)S(1)} %copy-done.13, f32[8,128,128]{2,1,0:T(8,128)S(1)} %copy-done.12, bf16[512,1024]{1,0:T(8,128)(2,1)S(1)} %copy-done), kind=kOutput, calls=%fused_computation.18 | convolution fusion | flops 806617088 | bytes 6291456 | tf_op jit(solution)/shard_map/nhde,nshe->nshd/dot_general | solution.py:78
  296.3 2.9 copy.53
  (27 shorter events, 0.2 us)
Async XLA Ops:
  7.2 2.3 copy-start
  7.2 58.4 %all-gather.8.cloned.1.call-start = ((), (), s32[]{:S(2)}) async-start(), calls=%async_computation.2 | async-start | bytes 4456448 | tf_op jit(solution)/shard_map/all_gather | solution.py:15
  9.5 1.4 copy-start.8
  9.5 1.9 copy-start.5
  10.9 146.1 %reduce-scatter.4.cloned.1.call-start = ((), (), s32[]{:S(2)}) async-start(), calls=%async_computation.4 | async-start | bytes 5898240
  65.6 1.0 copy-start.14
  96.7 0.7 copy-start.15
  96.7 105.4 %all-gather.6.cloned.1.call-start = ((), (), s32[]{:S(2)}) async-start(), calls=%async_computation.1 | async-start | bytes 5898240 | tf_op jit(solution)/shard_map/all_gather | solution.py:64
  161.6 106.0 %all-gather.10.cloned.1.call-start = ((), (), s32[]{:S(2)}) async-start(), calls=%async_computation.3 | async-start | bytes 4456448 | tf_op jit(solution)/shard_map/all_gather | solution.py:15
  202.1 11.3 %copy-start.6 = (bf16[512,1024]{1,0:T(8,128)(2,1)S(1)}, bf16[512,1024]{1,0:T(8,128)(2,1)}, u32[]{:S(2)}) copy-start(bf16[512,1024]{1,0:T(8,128)(2,1)} %param.10) | copy-start | bytes 3145732
  212.1 1.3 copy-start.2
  214.7 0.8 copy-start.11
  216.4 3.7 %copy-start.3 = (f32[512,1024]{0,1:T(8,128)S(1)}, f32[512,1024]{0,1:T(8,128)}, u32[]{:S(2)}) copy-start(f32[512,1024]{0,1:T(8,128)} %copy-done.2) | copy-start | bytes 6291460
  220.1 3.6 %copy-start.9 = (bf16[512,8,128]{0,2,1:T(8,128)(2,1)S(1)}, bf16[512,8,128]{0,2,1:T(8,128)(2,1)}, u32[]{:S(2)}) copy-start(bf16[512,8,128]{0,2,1:T(8,128)(2,1)} %copy-done.8) | copy-start | bytes 3145732
  223.7 6.7 %copy-start.1 = (f32[8,512,512]{2,1,0:T(8,128)}, f32[8,512,512]{2,1,0:T(8,128)S(1)}, u32[]{:S(2)}) copy-start(f32[8,512,512]{2,1,0:T(8,128)S(1)} %fusion.23) | copy-start | bytes 25165828
  230.3 3.0 copy-start.7
  233.3 8.4 %copy-start.4 = (f32[512,1024]{0,1:T(8,128)S(1)}, f32[512,1024]{0,1:T(8,128)}, u32[]{:S(2)}) copy-start(f32[512,1024]{0,1:T(8,128)} %copy-done.2) | copy-start | bytes 6291460
  267.6 17.6 %copy-start.10 = (bf16[512,1024]{1,0:T(8,128)(2,1)S(1)}, bf16[512,1024]{1,0:T(8,128)(2,1)}, u32[]{:S(2)}) copy-start(bf16[512,1024]{1,0:T(8,128)(2,1)} %param.11) | copy-start | bytes 3145732
  267.6 17.6 %copy-start.12 = (f32[8,128,128]{2,1,0:T(8,128)S(1)}, f32[8,128,128]{2,1,0:T(8,128)}, u32[]{:S(2)}) copy-start(f32[8,128,128]{2,1,0:T(8,128)} %copy-done.11) | copy-start | bytes 1572868
  289.3 2.9 copy-start.13
Sparse Core Ops, SparseCore 0:
  11.0 54.5 all-gather.7
  96.8 52.2 reduce-scatter.3
  161.7 40.3 all-gather.5
  216.5 50.9 all-gather.9
where the time goes:
time: 310 us; the launch traced here: 306 us
  waiting for transfers between devices  106 us (34%)
  matrix products  79.8 us (26%)
  blocking collectives  57.7 us (19%)
  local copies, waits for them, and re-layouts  27 us (9%)
  other arithmetic  19.3 us (6%)
  between operations  15.7 us (5%)
    all_gather x2, waiting for transfers between devices, entering(): gathered = lax.all_gather(x.astype(jnp.bfloat16), axis)  65.4 us
    psum x1, blocking collectives, on_device(): valid_total = lax.psum(count_local, 'ctx')  57.7 us
    all_gather x1, waiting for transfers between devices, on_device(): lax.all_gather(error_grad, 'head', axis=1, tiled=True)  40.5 us
    unnamed x38, local copies, waits for them, and re-layouts  24.4 us
    add x15, other arithmetic, add_states(): return earlier + later  16.2 us
    dot_general x1, matrix products, on_device(): terms = jnp.dot(attn, out_weight, preferred_element_type=jnp.float32)  11.4 us
    dot_general x1, matrix products, on_device(): lax.dot_general(lax.all_gather(error_grad, 'head', axis=1, tiled=True), o...  9.96 us
    dot_general x1, matrix products, on_device(): v_grad = jnp.einsum('nhts,nthe->nshe', scores, grad_f, precision=precise)  8.87 us
  transfers between devices with their start and end apart: 4, of which 3 were waited for; matrix products, arithmetic and copies ran while one was open for 13% of the time, Pallas kernels for 0%

commit v1 on v0

v1 whole, which is shorter than its diff:
```python
import functools
import math

import jax
import jax.numpy as jnp
from jax import lax
from jax.experimental import pallas as pl
from jax.experimental.pallas import tpu as pltpu
from jax.sharding import PartitionSpec as P

DH = 128
MESH = pl.DeviceIdType.MESH
F32 = jnp.float32
BF16 = jnp.bfloat16
NT = (((1,), (1,)), ((), ()))
TN = (((0,), (0,)), ((), ()))
NN = (((1,), (0,)), ((), ()))


def dot(a, b, dims):
    return lax.dot_general(a, b, dims, preferred_element_type=F32)


def lanes(start, size):
    return pl.ds(pl.multiple_of(start, 128), size)


def transfer(scale, heads, n_ctx, n_x, tokens,
             q_hbm, k_hbm, v_hbm, teacher_hbm, w_hbm, valid_ref,
             g_out, prefix_out, suffix_out,
             q, k, v, teacher, w, intra, attn, tp, trecv, relay_p, relay_m, fin_p, fin_m,
             gath, acc, g, loc, got, pre, state, loc2, got2, pre2, state2, cnt, cnts,
             in_sem, out_sem, a_s, a_r, b_s, b_r, c_s, c_r, d_s, d_r, n_s, n_r,
             t_s, t_r, x_s, x_r, gp_s, gp_r, gx_s, gx_r):
    rows = q.shape[0]
    half = rows // 2
    wide = w.shape[1] // n_x
    part = wide // 2
    me_c = lax.axis_index("ctx")
    me_h = lax.axis_index("head")
    x, core = me_h // 2, me_h % 2
    right = ((x + 1) % n_x) * 2 + core
    left = ((x + n_x - 1) % n_x) * 2 + core
    other = x * 2 + 1 - core
    pr = heads * DH // n_ctx

    barrier = pltpu.get_barrier_semaphore()
    for d in range(1, n_ctx):
        pl.semaphore_signal(barrier, inc=1, device_id=((me_c + d) % n_ctx, me_h), device_id_type=MESH)
    for h in (other, right, left):
        pl.semaphore_signal(barrier, inc=1, device_id=(me_c, h), device_id_type=MESH)

    loads = [
        pltpu.make_async_copy(src, dst, in_sem.at[i])
        for i, (src, dst) in enumerate(((k_hbm, k), (v_hbm, v), (q_hbm, q), (w_hbm, w), (teacher_hbm, teacher)))
    ]
    for one in loads:
        one.start()

    def peers(sending, src, dst, ssem, rsem, piece):
        out = []
        for d in range(1, n_ctx):
            peer = (me_c + d) % n_ctx if sending else (me_c + n_ctx - d) % n_ctx
            place = me_c if sending else peer
            out.append(pltpu.make_async_remote_copy(
                src_ref=src.at[pl.ds(pl.multiple_of(peer * piece, piece), piece)] if src is not cnt else src,
                dst_ref=dst.at[pl.ds(pl.multiple_of(place * piece, piece), piece)],
                send_sem=ssem.at[d],
                recv_sem=rsem.at[place],
                device_id=(peer, me_h),
                device_id_type=MESH,
            ))
        return out

    def mine(piece):
        return pl.ds(pl.multiple_of(me_c * piece, piece), piece)

    def scan(got_ref, pre_ref, backward):
        total = jnp.zeros((pr, DH), F32)
        order = range(n_ctx - 1, -1, -1) if backward else range(n_ctx)
        for j in order:
            block = slice(j * pr, (j + 1) * pr)
            pre_ref[block, :] = total.astype(BF16)
            total = total + got_ref[block, :].astype(F32)

    def start(copies):
        for one in copies:
            one.start()

    def finish_recv(copies):
        for one in copies:
            one.wait_recv()

    def finish_send(copies):
        for one in copies:
            one.wait_send()

    loads[0].wait()
    loads[1].wait()

    @pl.loop(0, heads)
    def _(h):
        cols = lanes(h * DH, DH)
        loc[pl.ds(pl.multiple_of(h * DH, DH), DH), :] = dot(k[:, cols], v[:, cols], TN).astype(BF16)

    cnt[...] = jnp.zeros_like(cnt) + jnp.sum(valid_ref[...])
    pl.semaphore_wait(barrier, n_ctx - 1 + 3)

    a_send = peers(True, loc, got, a_s, a_r, pr)
    n_send = peers(True, cnt, cnts, n_s, n_r, 8)
    start(a_send)
    start(n_send)
    got[mine(pr), :] = loc[mine(pr), :]
    cnts[mine(8), :] = cnt[...]

    loads[2].wait()
    row = lax.broadcasted_iota(jnp.int32, (half, half), 0)
    col = lax.broadcasted_iota(jnp.int32, (half, half), 1)
    lower = row >= col

    @pl.loop(0, heads)
    def _(h):
        cols = lanes(h * DH, DH)
        k0, k1 = k[0:half, cols], k[half:rows, cols]
        v0, v1 = v[0:half, cols], v[half:rows, cols]
        q0, q1 = q[0:half, cols], q[half:rows, cols]
        s0 = jnp.where(lower, dot(q0, k0, NT), 0.0).astype(BF16)
        intra[0:half, cols] = dot(s0, v0, NN)
        s10 = dot(q1, k0, NT).astype(BF16)
        s11 = jnp.where(lower, dot(q1, k1, NT), 0.0).astype(BF16)
        intra[half:rows, cols] = dot(s10, v0, NN) + dot(s11, v1, NN)

    finish_recv(peers(False, loc, got, a_s, a_r, pr))
    scan(got, pre, False)
    b_send = peers(True, pre, state, b_s, b_r, pr)
    start(b_send)
    state[mine(pr), :] = pre[mine(pr), :]
    finish_send(a_send)
    finish_send(n_send)
    finish_recv(peers(False, cnt, cnts, n_s, n_r, 8))
    count = cnts[0:8, :]
    for j in range(1, n_ctx):
        count = count + cnts[j * 8 : j * 8 + 8, :]
    cnt[...] = tokens / count
    loads[3].wait()
    loads[4].wait()
    finish_recv(peers(False, pre, state, b_s, b_r, pr))

    @pl.loop(0, heads)
    def _(h):
        cols = lanes(h * DH, DH)
        carried = dot(q[:, cols], state[pl.ds(pl.multiple_of(h * DH, DH), DH), :], NN)
        attn[:, cols] = (scale * (intra[:, cols] + carried)).astype(BF16)

    def remote(src, dst, ssem, rsem, device):
        return pltpu.make_async_remote_copy(
            src_ref=src, dst_ref=dst, send_sem=ssem, recv_sem=rsem,
            device_id=(me_c, device), device_id_type=MESH)

    own = lanes(core * part, part)
    theirs = lanes((1 - core) * part, part)
    first, second = pl.ds(0, half), pl.ds(half, half)
    step_rows = 64

    t_copies, x_copies = [], []
    targets = [(x + 2) % n_x, (x + 1) % n_x, (x + 3) % n_x, x]

    def terms(i):
        base = targets[i] * wide

        @pl.loop(0, wide // 256)
        def _(n):
            tp[i, :, lanes(n * 256, 256)] = dot(attn[...], w[:, lanes(base + n * 256, 256)], NN).astype(BF16)

        copy = remote(tp.at[i, :, theirs], trecv.at[i], t_s.at[i], t_r.at[i], other)
        copy.start()
        t_copies.append(copy)

    def add_chip(i):
        t_copies[i].wait_recv()

        @pl.loop(0, rows // step_rows)
        def _(r):
            at = pl.ds(pl.multiple_of(r * step_rows, step_rows), step_rows)
            tp[i, at, own] = (tp[i, at, own].astype(F32) + trecv[i, at, :].astype(F32)).astype(BF16)

    def add_relay(i, rel, base):
        @pl.loop(0, half // step_rows)
        def _(r):
            off = pl.multiple_of(r * step_rows, step_rows)
            at = pl.ds(base + off, step_rows)
            tp[i, at, own] = (tp[i, at, own].astype(F32) + rel[pl.ds(off, step_rows), :].astype(F32)).astype(BF16)

    def send_x(n, src, dst, device):
        copy = remote(src, dst, x_s.at[n], x_r.at[n], device)
        copy.start()
        x_copies.append(copy)

    terms(0)
    terms(1)
    add_chip(0)
    send_x(0, tp.at[0, first, own], relay_p, right)
    send_x(1, tp.at[0, second, own], relay_m, left)
    terms(2)
    add_chip(1)
    send_x(2, tp.at[1, second, own], fin_p.at[second], right)
    terms(3)
    add_chip(2)
    send_x(3, tp.at[2, first, own], fin_m.at[first], left)
    x_copies[0].wait_recv()
    add_relay(1, relay_p, 0)
    send_x(4, tp.at[1, first, own], fin_p.at[first], right)
    x_copies[1].wait_recv()
    add_relay(2, relay_m, half)
    send_x(5, tp.at[2, second, own], fin_m.at[second], left)
    t_copies[3].wait_recv()

    def error(base):
        @pl.loop(0, half // step_rows)
        def _(r):
            at = pl.ds(pl.multiple_of(base + r * step_rows, step_rows), step_rows)
            pred = tp[3, at, own].astype(F32) + trecv[3, at, :].astype(F32)
            pred = pred + fin_p[at, :].astype(F32) + fin_m[at, :].astype(F32)
            miss = pred - teacher[at, :].astype(F32)
            gath[x, at, own] = (valid_ref[at, :] * miss * cnt[0:1, 0:1]).astype(BF16)

    gp_copies, gx_copies = {}, {}

    def to_other(n, block, at):
        ref = gath.at[block, at, own]
        copy = remote(ref, ref, gp_s.at[n], gp_r.at[n], other)
        copy.start()
        gp_copies[n] = copy

    def from_other(n, block, at):
        ref = gath.at[block, at, theirs]
        remote(ref, ref, gp_s.at[n], gp_r.at[n], other).wait_recv()

    def to_x(n, block, at, device):
        ref = gath.at[block, at, own]
        copy = remote(ref, ref, gx_s.at[n], gx_r.at[n], device)
        copy.start()
        gx_copies[n] = copy

    def from_x(n, block, at, device):
        ref = gath.at[block, at, own]
        remote(ref, ref, gx_s.at[n], gx_r.at[n], device).wait_recv()

    far, near_l, near_r = (x + 2) % n_x, (x + 3) % n_x, (x + 1) % n_x
    x_copies[3].wait_recv()
    x_copies[4].wait_recv()
    error(0)
    to_x(0, x, first, right)
    to_other(0, x, first)
    x_copies[2].wait_recv()
    x_copies[5].wait_recv()
    error(half)
    to_x(1, x, second, left)
    to_x(2, x, second, right)
    to_x(3, x, first, left)
    to_other(1, x, second)

    def contract(block, base, fresh=False):
        @pl.loop(0, heads * DH // 256)
        def _(n):
            at = pl.ds(base, half)
            cols = lanes(n * 256, 256)
            new = dot(
                gath[block, at, :],
                w[pl.ds(pl.multiple_of(n * 256, 256), 256), lanes(block * wide, wide)],
                NT,
            )
            acc[at, cols] = new if fresh else acc[at, cols] + new

    from_other(0, x, first)
    contract(x, 0, True)
    from_x(0, near_l, first, left)
    to_x(4, near_l, first, right)
    to_other(2, near_l, first)
    from_x(1, near_r, second, right)
    to_x(5, near_r, second, left)
    to_other(3, near_r, second)
    from_other(1, x, second)
    contract(x, half, True)
    from_other(2, near_l, first)
    contract(near_l, 0)
    from_other(3, near_r, second)
    contract(near_r, half)
    from_x(2, near_l, second, left)
    to_other(4, near_l, second)
    from_x(3, near_r, first, right)
    to_other(5, near_r, first)
    from_other(4, near_l, second)
    contract(near_l, half)
    from_other(5, near_r, first)
    contract(near_r, 0)
    from_x(4, far, first, left)
    to_other(6, far, first)
    from_x(5, far, second, right)
    to_other(7, far, second)
    from_other(6, far, first)
    contract(far, 0)
    from_other(7, far, second)
    contract(far, half)

    @pl.loop(0, heads)
    def _(h):
        cols = lanes(h * DH, DH)
        g_h = acc[:, cols].astype(BF16)
        g[:, cols] = g_h
        loc2[pl.ds(pl.multiple_of(h * DH, DH), DH), :] = dot(q[:, cols], g_h, TN).astype(BF16)

    c_send = peers(True, loc2, got2, c_s, c_r, pr)
    start(c_send)
    got2[mine(pr), :] = loc2[mine(pr), :]
    outs = [
        pltpu.make_async_copy(g, g_out, out_sem.at[0]),
        pltpu.make_async_copy(state, prefix_out, out_sem.at[1]),
    ]
    start(outs)
    finish_send(b_send)
    finish_send(t_copies)
    finish_send(x_copies)
    finish_send(gp_copies.values())
    finish_send(gx_copies.values())
    finish_recv(peers(False, loc2, got2, c_s, c_r, pr))
    scan(got2, pre2, True)
    d_send = peers(True, pre2, state2, d_s, d_r, pr)
    start(d_send)
    state2[mine(pr), :] = pre2[mine(pr), :]
    finish_send(c_send)
    finish_recv(peers(False, pre2, state2, d_s, d_r, pr))
    last = pltpu.make_async_copy(state2, suffix_out, out_sem.at[2])
    last.start()
    finish_send(d_send)
    for one in outs:
        one.wait()
    last.wait()


def gradients(scale, per, q_ref, k_ref, v_ref, g_ref, p_ref, r_ref, dq_ref, dk_ref, dv_ref):
    rows = q_ref.shape[0]
    half = rows // 2
    row = lax.broadcasted_iota(jnp.int32, (half, half), 0)
    col = lax.broadcasted_iota(jnp.int32, (half, half), 1)
    lower = row >= col
    upper = row <= col
    for h in range(per):
        cols = slice(h * DH, (h + 1) * DH)
        q0, q1 = q_ref[0:half, cols], q_ref[half:rows, cols]
        k0, k1 = k_ref[0:half, cols], k_ref[half:rows, cols]
        v0, v1 = v_ref[0:half, cols], v_ref[half:rows, cols]
        g0, g1 = g_ref[0:half, cols], g_ref[half:rows, cols]
        p, r = p_ref[cols, :], r_ref[cols, :]

        def tri(a, b, mask):
            return jnp.where(mask, dot(a, b, NT), 0.0).astype(BF16)

        def full(a, b):
            return dot(a, b, NT).astype(BF16)

        dq_ref[0:half, cols] = scale * (dot(tri(g0, v0, lower), k0, NN) + dot(g0, p, NT))
        dq_ref[half:rows, cols] = scale * (
            dot(full(g1, v0), k0, NN) + dot(tri(g1, v1, lower), k1, NN) + dot(g1, p, NT)
        )
        dk_ref[0:half, cols] = scale * (
            dot(tri(v0, g0, upper), q0, NN) + dot(full(v0, g1), q1, NN) + dot(v0, r, NT)
        )
        dk_ref[half:rows, cols] = scale * (dot(tri(v1, g1, upper), q1, NN) + dot(v1, r, NT))
        dv_ref[0:half, cols] = scale * (
            dot(tri(k0, q0, upper), g0, NN) + dot(full(k0, q1), g1, NN) + dot(k0, r, NN)
        )
        dv_ref[half:rows, cols] = scale * (dot(tri(k1, q1, upper), g1, NN) + dot(k1, r, NN))


def on_device(queries, keys, values, teacher, out_weight, valid):
    rows, width = queries.shape
    heads = width // DH
    model = out_weight.shape[1]
    n_ctx = lax.axis_size("ctx")
    n_x = lax.axis_size("head") // 2
    half = rows // 2
    wide = model // n_x
    part = wide // 2
    tokens = float(rows * n_ctx)
    scale = 1.0 / math.sqrt(DH * rows * n_ctx)
    valid_col = valid.astype(F32).reshape(rows, 1)
    anywhere = pl.BlockSpec(memory_space=pl.ANY)
    vmem = pl.BlockSpec(memory_space=pltpu.VMEM)
    dma = pltpu.SemaphoreType.DMA
    st = lambda: pltpu.VMEM((heads * DH, DH), BF16)
    g, prefix, suffix = pl.pallas_call(
        functools.partial(transfer, scale, heads, n_ctx, n_x, tokens),
        name="transfer",
        out_shape=(
            jax.ShapeDtypeStruct((rows, width), BF16),
            jax.ShapeDtypeStruct((width, DH), BF16),
            jax.ShapeDtypeStruct((width, DH), BF16),
        ),
        in_specs=[anywhere] * 5 + [vmem],
        out_specs=(anywhere,) * 3,
        scratch_shapes=[
            pltpu.VMEM((rows, width), BF16),
            pltpu.VMEM((rows, width), BF16),
            pltpu.VMEM((rows, width), BF16),
            pltpu.VMEM((rows, part), BF16),
            pltpu.VMEM((width, model), BF16),
            pltpu.VMEM((rows, width), F32),
            pltpu.VMEM((rows, width), BF16),
            pltpu.VMEM((4, rows, wide), BF16),
            pltpu.VMEM((4, rows, part), BF16),
            pltpu.VMEM((half, part), BF16),
            pltpu.VMEM((half, part), BF16),
            pltpu.VMEM((rows, part), BF16),
            pltpu.VMEM((rows, part), BF16),
            pltpu.VMEM((n_x, rows, wide), BF16),
            pltpu.VMEM((rows, width), F32),
            pltpu.VMEM((rows, width), BF16),
            st(), st(), st(), st(), st(), st(), st(), st(),
            pltpu.VMEM((8, 128), F32),
            pltpu.VMEM((8 * n_ctx, 128), F32),
            dma((5,)), dma((3,)),
            dma((n_ctx,)), dma((n_ctx,)), dma((n_ctx,)), dma((n_ctx,)),
            dma((n_ctx,)), dma((n_ctx,)), dma((n_ctx,)), dma((n_ctx,)),
            dma((n_ctx,)), dma((n_ctx,)),
            dma((4,)), dma((4,)), dma((6,)), dma((6,)),
            dma((8,)), dma((8,)), dma((6,)), dma((6,)),
        ],
        compiler_params=pltpu.CompilerParams(
            collective_id=0, has_side_effects=True, vmem_limit_bytes=60 * 1024 * 1024
        ),
    )(queries, keys, values, teacher, out_weight, valid_col)

    per = 2
    block = pl.BlockSpec((rows, per * DH), lambda i: (0, i))
    square = pl.BlockSpec((per * DH, DH), lambda i: (i, 0))
    out = jax.ShapeDtypeStruct((rows, width), F32)
    return tuple(pl.pallas_call(
        functools.partial(gradients, scale, per),
        name="gradients",
        grid=(heads // per,),
        out_shape=(out, out, out),
        in_specs=[block] * 4 + [square] * 2,
        out_specs=(block,) * 3,
    )(queries, keys, values, g, prefix, suffix))


def solution(mesh):
    in_specs = (
        P("ctx", "head"),
        P("ctx", "head"),
        P("ctx", "head"),
        P("ctx", "head"),
        P("head", None),
        P("ctx"),
    )
    out_specs = (P("ctx", "head"), P("ctx", "head"), P("ctx", "head"))
    return jax.shard_map(
        on_device, mesh=mesh, in_specs=in_specs, out_specs=out_specs, check_vma=False
    )
```

time: 310 us -> 109 us (0.35); the launches traced: 306 us -> 108 us
  Pallas kernels: 0 us -> 106 us
  waiting for transfers between devices: 106 us -> 0 us
  matrix products: 79.8 us -> 0 us
  blocking collectives: 57.7 us -> 0 us
  local copies, waits for them, and re-layouts: 27 us -> 0.86 us
  other arithmetic: 19.3 us -> 0.68 us
  between operations: 15.7 us -> 0.64 us
    pallas_call x0 -> x2, Pallas kernels: none -> 106 us  [the longest x1 94.2 us: on_device(): pl.pallas_call(functools.partial(transfer, scale, heads, n_ctx, n_x, toke...]
    all_gather x3 -> x0, waiting for transfers between devices: 106 us -> none  [the longest x2 65.4 us: entering(): gathered = lax.all_gather(x.astype(jnp.bfloat16), axis)]
    dot_general x14 -> x0, matrix products: 79.8 us -> none  [the longest x1 11.4 us: on_device(): terms = jnp.dot(attn, out_weight, preferred_element_type=jnp.float32)]
    psum x1 -> x0, blocking collectives: 57.7 us -> none  [on_device(): valid_total = lax.psum(count_local, 'ctx')]
    unnamed x38 -> x0, local copies, waits for them, and re-layouts: 24.4 us -> none
    add x15 -> x0, other arithmetic: 16.2 us -> none  [add_states(): return earlier + later]
  transfers between devices with their start and end apart: 4 -> 0, of which waited for: 3 -> 0; matrix products, arithmetic and copies ran while one was open for 13% -> 0% of each run, Pallas kernels for 0% -> 0%
where the time goes in v1:
time: 109 us; the launch traced here: 108 us
  Pallas kernels  106 us (97%)
    pallas_call x1, Pallas kernels, on_device(): pl.pallas_call(functools.partial(transfer, scale, heads, n_ctx, n_x, toke...  94.2 us
    pallas_call x1, Pallas kernels, on_device(): pl.pallas_call(functools.partial(gradients, scale, per), name='gradients'...  11.9 us

profile of v1, /device:TPU:1, one launch (start us, length us, event | category | flops | bytes accessed | tf_op | source)
XLA Modules:
  0.0 108.3 jit_solution(10882707854384456407)
XLA Ops:
  0.6 0.7 convert_element_type.3
  1.3 0.9 copy.9.valid_ref
  2.2 94.2 %transfer.1 = (bf16[512,1024]{1,0:T(8,128)(2,1)}, bf16[1024,128]{1,0:T(8,128)(2,1)}, bf16[1024,128]{1,0:T(8,128)(2,1)}) custom-call(bf16[512,1024]{1,0:T(8,128)(2,1)} %q_ref.1, bf16[512,1024]{1,0:T(8,128)(2,1)} %k_ref.1, bf16[512,1024]{1,0:T(8,128)(2,1)} %v_ref.1, bf16[512,640]{1,0:T(8,128)(2,1)} %teacher_hbm.1, bf16[1024,5120]{1,0:T(8,128)(2,1)} %w_hbm.1, ...), custom_call_target="tpu_custom_call" | custom-call | tf_op jit(solution)/shard_map/transfer/pallas_call | solution.py:392
  96.4 11.9 %gradients.1 = (f32[512,1024]{1,0:T(8,128)}, f32[512,1024]{1,0:T(8,128)}, f32[512,1024]{1,0:T(8,128)}) custom-call(bf16[512,1024]{1,0:T(8,128)(2,1)} %q_ref.1, bf16[512,1024]{1,0:T(8,128)(2,1)} %k_ref.1, bf16[512,1024]{1,0:T(8,128)(2,1)} %v_ref.1, bf16[512,1024]{1,0:T(8,128)(2,1)} %get-tuple-element.6.g_ref, bf16[1024,128]{1,0:T(8,128)(2,1)} %get-tuple-element.7.p_ref, ...), custom_call_target="tpu_custom_call" | custom-call | tf_op jit(solution)/shard_map/gradients/pallas_call | solution.py:438

commit v2 on v1

v2 whole, which is shorter than its diff:
```python
import functools
import math

import jax
import jax.numpy as jnp
from jax import lax
from jax.experimental import pallas as pl
from jax.experimental.pallas import tpu as pltpu
from jax.sharding import PartitionSpec as P

DH = 128
MESH = pl.DeviceIdType.MESH
F32 = jnp.float32
BF16 = jnp.bfloat16
NT = (((1,), (1,)), ((), ()))
TN = (((0,), (0,)), ((), ()))
NN = (((1,), (0,)), ((), ()))


def dot(a, b, dims):
    return lax.dot_general(a, b, dims, preferred_element_type=F32)


def lanes(start, size):
    return pl.ds(pl.multiple_of(start, 128), size)


def transfer(scale, heads, n_ctx, n_x, tokens,
             q_hbm, k_hbm, v_hbm, teacher_hbm, w_hbm, valid_ref,
             dq_out, dk_out, dv_out, suffix_out,
             q, k, v, teacher, w, intra, attn, tp, trecv, relay_p, relay_m, fin_p, fin_m,
             gath, acc, g, dk, dv, weight, loc, got, pre, state, loc2, got2, pre2, state2, cnt, cnts,
             in_sem, out_sem, a_s, a_r, b_s, b_r, c_s, c_r, d_s, d_r, n_s, n_r,
             t_s, t_r, x_s, x_r, gp_s, gp_r, gx_s, gx_r):
    dq = intra
    rows = q.shape[0]
    half = rows // 2
    quarter = rows // 4
    wide = w.shape[1] // n_x
    part = wide // 2
    me_c = lax.axis_index("ctx")
    me_h = lax.axis_index("head")
    x, core = me_h // 2, me_h % 2
    right = ((x + 1) % n_x) * 2 + core
    left = ((x + n_x - 1) % n_x) * 2 + core
    other = x * 2 + 1 - core
    pr = heads * DH // n_ctx

    barrier = pltpu.get_barrier_semaphore()
    for d in range(1, n_ctx):
        pl.semaphore_signal(barrier, inc=1, device_id=((me_c + d) % n_ctx, me_h), device_id_type=MESH)
    for h in (other, right, left):
        pl.semaphore_signal(barrier, inc=1, device_id=(me_c, h), device_id_type=MESH)

    loads = [
        pltpu.make_async_copy(src, dst, in_sem.at[i])
        for i, (src, dst) in enumerate(((k_hbm, k), (v_hbm, v), (q_hbm, q), (w_hbm, w), (teacher_hbm, teacher)))
    ]
    for one in loads[:3]:
        one.start()

    def peers(sending, src, dst, ssem, rsem, piece):
        out = []
        for d in range(1, n_ctx):
            peer = (me_c + d) % n_ctx if sending else (me_c + n_ctx - d) % n_ctx
            place = me_c if sending else peer
            out.append(pltpu.make_async_remote_copy(
                src_ref=src.at[pl.ds(pl.multiple_of(peer * piece, piece), piece)] if src is not cnt else src,
                dst_ref=dst.at[pl.ds(pl.multiple_of(place * piece, piece), piece)],
                send_sem=ssem.at[d],
                recv_sem=rsem.at[place],
                device_id=(peer, me_h),
                device_id_type=MESH,
            ))
        return out

    def mine(piece):
        return pl.ds(pl.multiple_of(me_c * piece, piece), piece)

    def head_rows(h):
        return pl.ds(pl.multiple_of(h * DH, DH), DH)

    def scan(got_ref, pre_ref, backward):
        total = jnp.zeros((pr, DH), F32)
        order = range(n_ctx - 1, -1, -1) if backward else range(n_ctx)
        for j in order:
            block = slice(j * pr, (j + 1) * pr)
            pre_ref[block, :] = total.astype(BF16)
            total = total + got_ref[block, :].astype(F32)

    def start(copies):
        for one in copies:
            one.start()

    def finish_recv(copies):
        for one in copies:
            one.wait_recv()

    def finish_send(copies):
        for one in copies:
            one.wait_send()

    loads[0].wait()
    loads[1].wait()

    @pl.loop(0, heads)
    def _(h):
        cols = lanes(h * DH, DH)
        loc[head_rows(h), :] = dot(k[:, cols], v[:, cols], TN).astype(BF16)

    loads[3].start()
    loads[4].start()
    flags = valid_ref[...].astype(F32)
    cnt[...] = jnp.zeros_like(cnt) + jnp.sum(flags)
    pl.semaphore_wait(barrier, n_ctx - 1 + 3)

    a_send = peers(True, loc, got, a_s, a_r, pr)
    n_send = peers(True, cnt, cnts, n_s, n_r, 8)
    start(a_send)
    start(n_send)
    got[mine(pr), :] = loc[mine(pr), :]
    cnts[mine(8), :] = cnt[...]

    loads[2].wait()
    row = lax.broadcasted_iota(jnp.int32, (half, half), 0)
    col = lax.broadcasted_iota(jnp.int32, (half, half), 1)
    lower = row >= col
    upper = row <= col

    def both(ref, cols):
        return ref[0:half, cols], ref[half:rows, cols]

    def full(a, b):
        return dot(a, b, NT).astype(BF16)

    def tri(a, b, mask):
        return jnp.where(mask, dot(a, b, NT), 0.0).astype(BF16)

    @pl.loop(0, heads)
    def _(h):
        cols = lanes(h * DH, DH)
        (k0, k1), (v0, v1), (q0, q1) = both(k, cols), both(v, cols), both(q, cols)
        intra[0:half, cols] = dot(tri(q0, k0, lower), v0, NN)
        intra[half:rows, cols] = dot(full(q1, k0), v0, NN) + dot(tri(q1, k1, lower), v1, NN)

    finish_recv(peers(False, loc, got, a_s, a_r, pr))
    scan(got, pre, False)
    b_send = peers(True, pre, state, b_s, b_r, pr)
    start(b_send)
    state[mine(pr), :] = pre[mine(pr), :]
    finish_send(a_send)
    finish_send(n_send)
    finish_recv(peers(False, cnt, cnts, n_s, n_r, 8))
    count = cnts[0:8, :]
    for j in range(1, n_ctx):
        count = count + cnts[j * 8 : j * 8 + 8, :]
    factor = (tokens / count)[0:1, :]
    diagonal = row[0:DH, 0:DH] == col[0:DH, 0:DH]
    for j in range(rows // DH):
        column = jnp.sum(jnp.where(diagonal, flags[j : j + 1, :], 0.0), axis=1, keepdims=True)
        weight[j * DH : (j + 1) * DH, :] = column * factor
    loads[3].wait()
    loads[4].wait()
    finish_recv(peers(False, pre, state, b_s, b_r, pr))

    def attend(base):
        at = pl.ds(base, half)

        @pl.loop(0, heads)
        def _(h):
            cols = lanes(h * DH, DH)
            carried = dot(q[at, cols], state[head_rows(h), :], NN)
            attn[at, cols] = (scale * (intra[at, cols] + carried)).astype(BF16)

    def remote(src, dst, ssem, rsem, device):
        return pltpu.make_async_remote_copy(
            src_ref=src, dst_ref=dst, send_sem=ssem, recv_sem=rsem,
            device_id=(me_c, device), device_id_type=MESH)

    own = lanes(core * part, part)
    theirs = lanes((1 - core) * part, part)
    step_rows = 64
    sent = []

    def send(src, dst, ssem, rsem, n, device):
        copy = remote(src, dst, ssem.at[n], rsem.at[n], device)
        copy.start()
        sent.append(copy)
        return copy

    def quarters(c):
        return pl.ds(2 * c * quarter, quarter), pl.ds((2 * c + 1) * quarter, quarter)

    near_r, near_l, far = (x + 1) % n_x, (x + n_x - 1) % n_x, (x + 2) % n_x
    targets = [far, near_r, near_l, x]
    t_copies, x_copies = {}, {}

    def terms(i, c):
        at = pl.ds(c * half, half)
        base = targets[i] * wide

        @pl.loop(0, wide // 256)
        def _(n):
            tp[i, at, lanes(n * 256, 256)] = dot(attn[at, :], w[:, lanes(base + n * 256, 256)], NN).astype(BF16)

        t_copies[i, c] = send(tp.at[i, at, theirs], trecv.at[i, at, :], t_s, t_r, 4 * c + i, other)

    def add_chip(i, c):
        t_copies[i, c].wait_recv()

        @pl.loop(0, half // step_rows)
        def _(r):
            at = pl.ds(pl.multiple_of(c * half + r * step_rows, step_rows), step_rows)
            tp[i, at, own] = (tp[i, at, own].astype(F32) + trecv[i, at, :].astype(F32)).astype(BF16)

    def add_relay(i, rel, c, base):
        @pl.loop(0, quarter // step_rows)
        def _(r):
            off = pl.multiple_of(r * step_rows, step_rows)
            at = pl.ds(base + off, step_rows)
            tp[i, at, own] = (tp[i, at, own].astype(F32) + rel[c, pl.ds(off, step_rows), :].astype(F32)).astype(BF16)

    def send_x(n, c, src, dst, device):
        x_copies[n, c] = send(src, dst, x_s, x_r, 6 * c + n, device)

    def far_out(c):
        qa, qb = quarters(c)
        add_chip(0, c)
        send_x(0, c, tp.at[0, qa, own], relay_p.at[c], right)
        send_x(1, c, tp.at[0, qb, own], relay_m.at[c], left)

    def right_out(c):
        qa, qb = quarters(c)
        add_chip(1, c)
        send_x(2, c, tp.at[1, qb, own], fin_p.at[qb], right)

    def left_out(c):
        qa, qb = quarters(c)
        add_chip(2, c)
        send_x(3, c, tp.at[2, qa, own], fin_m.at[qa], left)

    def relayed(c):
        qa, qb = quarters(c)
        x_copies[0, c].wait_recv()
        add_relay(1, relay_p, c, 2 * c * quarter)
        send_x(4, c, tp.at[1, qa, own], fin_p.at[qa], right)
        x_copies[1, c].wait_recv()
        add_relay(2, relay_m, c, (2 * c + 1) * quarter)
        send_x(5, c, tp.at[2, qb, own], fin_m.at[qb], left)

    def to_other(n, c, block, at):
        ref = gath.at[block, at, own]
        send(ref, ref, gp_s, gp_r, 7 * c + n, other)

    def from_other(n, c, block, at):
        ref = gath.at[block, at, theirs]
        remote(ref, ref, gp_s.at[7 * c + n], gp_r.at[7 * c + n], other).wait_recv()

    def to_x(n, c, block, at, device):
        ref = gath.at[block, at, own]
        send(ref, ref, gx_s, gx_r, 6 * c + n, device)

    def from_x(n, c, block, at, device):
        ref = gath.at[block, at, own]
        remote(ref, ref, gx_s.at[6 * c + n], gx_r.at[6 * c + n], device).wait_recv()

    def error(c):
        t_copies[3, c].wait_recv()
        for n in (2, 3, 4, 5):
            x_copies[n, c].wait_recv()

        @pl.loop(0, half // step_rows)
        def _(r):
            at = pl.ds(pl.multiple_of(c * half + r * step_rows, step_rows), step_rows)
            pred = tp[3, at, own].astype(F32) + trecv[3, at, :].astype(F32)
            pred = pred + fin_p[at, :].astype(F32) + fin_m[at, :].astype(F32)
            miss = pred - teacher[at, :].astype(F32)
            gath[x, at, own] = (miss * jnp.concatenate([weight[at, :]] * (part // DH), axis=1)).astype(BF16)

        qa, qb = quarters(c)
        to_x(0, c, x, qa, right)
        to_x(1, c, x, qb, left)
        to_x(2, c, x, qb, right)
        to_x(3, c, x, qa, left)
        to_other(0, c, x, pl.ds(c * half, half))

    def near_first(c):
        qa, qb = quarters(c)
        from_x(0, c, near_l, qa, left)
        to_x(4, c, near_l, qa, right)
        to_other(1, c, near_l, qa)
        from_x(1, c, near_r, qb, right)
        to_x(5, c, near_r, qb, left)
        to_other(2, c, near_r, qb)

    def near_second(c):
        qa, qb = quarters(c)
        from_x(2, c, near_l, qb, left)
        to_other(3, c, near_l, qb)
        from_x(3, c, near_r, qa, right)
        to_other(4, c, near_r, qa)

    def far_in(c):
        qa, qb = quarters(c)
        from_x(4, c, far, qa, left)
        to_other(5, c, far, qa)
        from_x(5, c, far, qb, right)
        to_other(6, c, far, qb)

    def contract(block, c, lo=0, size=wide, fresh=False):
        at = pl.ds(c * half, half)

        @pl.loop(0, heads * DH // 256)
        def _(n):
            cols = lanes(n * 256, 256)
            new = dot(
                gath[block, at, lanes(lo, size)],
                w[lanes(n * 256, 256), lanes(block * wide + lo, size)],
                NT,
            )
            acc[at, cols] = new if fresh else acc[at, cols] + new

    def contract_own(c):
        from_other(0, c, x, pl.ds(c * half, half))
        contract(x, c, fresh=True)

    def contract_near(c):
        qa, qb = quarters(c)
        from_other(1, c, near_l, qa)
        from_other(3, c, near_l, qb)
        contract(near_l, c)
        from_other(2, c, near_r, qb)
        from_other(4, c, near_r, qa)
        contract(near_r, c)

    def contract_far(c):
        qa, qb = quarters(c)
        contract(far, c, core * part, part)
        from_other(5, c, far, qa)
        from_other(6, c, far, qb)
        contract(far, c, (1 - core) * part, part)

    attend(0)
    terms(0, 0)
    terms(1, 0)
    far_out(0)
    terms(2, 0)
    right_out(0)
    terms(3, 0)
    left_out(0)
    attend(half)
    terms(0, 1)
    relayed(0)
    terms(1, 1)
    far_out(1)
    terms(2, 1)
    right_out(1)
    terms(3, 1)
    left_out(1)
    error(0)
    relayed(1)
    contract_own(0)
    near_first(0)
    near_second(0)
    contract_near(0)
    error(1)
    contract_own(1)
    far_in(0)
    contract_far(0)

    @pl.loop(0, heads)
    def _(h):
        cols = lanes(h * DH, DH)
        g_h = acc[0:half, cols].astype(BF16)
        g[0:half, cols] = g_h
        acc[0:DH, cols] = dot(q[0:half, cols], g_h, TN)

    near_first(1)

    @pl.loop(0, heads)
    def _(h):
        cols = lanes(h * DH, DH)
        k0, v0, q0, g0 = k[0:half, cols], v[0:half, cols], q[0:half, cols], g[0:half, cols]
        dq[0:half, cols] = dot(tri(g0, v0, lower), k0, NN) + dot(g0, state[head_rows(h), :], NT)
        dk[0:half, cols] = dot(tri(v0, g0, upper), q0, NN)
        dv[0:half, cols] = dot(tri(k0, q0, upper), g0, NN)

    near_second(1)
    contract_near(1)
    far_in(1)
    contract_far(1)

    @pl.loop(0, heads)
    def _(h):
        cols = lanes(h * DH, DH)
        g_h = acc[half:rows, cols].astype(BF16)
        g[half:rows, cols] = g_h
        loc2[head_rows(h), :] = (acc[0:DH, cols] + dot(q[half:rows, cols], g_h, TN)).astype(BF16)

    c_send = peers(True, loc2, got2, c_s, c_r, pr)
    start(c_send)
    got2[mine(pr), :] = loc2[mine(pr), :]

    outs = []

    def second_half(lo, hi):
        @pl.loop(lo, hi)
        def _(h):
            cols = lanes(h * DH, DH)
            (k0, k1), (v0, v1), (q0, q1) = both(k, cols), both(v, cols), both(q, cols)
            g1 = g[half:rows, cols]
            dq[half:rows, cols] = (
                dot(full(g1, v0), k0, NN) + dot(tri(g1, v1, lower), k1, NN)
                + dot(g1, state[head_rows(h), :], NT)
            )
            dk[0:half, cols] += dot(full(v0, g1), q1, NN)
            dk[half:rows, cols] = dot(tri(v1, g1, upper), q1, NN)
            dv[0:half, cols] += dot(full(k0, q1), g1, NN)
            dv[half:rows, cols] = dot(tri(k1, q1, upper), g1, NN)

        cols = pl.ds(lo * DH, (hi - lo) * DH)
        for src, dst in ((dq, dq_out), (dk, dk_out), (dv, dv_out)):
            copy = pltpu.make_async_copy(src.at[:, cols], dst.at[:, cols], out_sem.at[len(outs)])
            copy.start()
            outs.append(copy)

    second_half(0, heads // 2)
    finish_recv(peers(False, loc2, got2, c_s, c_r, pr))
    scan(got2, pre2, True)
    d_send = peers(True, pre2, state2, d_s, d_r, pr)
    start(d_send)
    state2[mine(pr), :] = pre2[mine(pr), :]
    second_half(heads // 2, heads)
    finish_send(b_send)
    finish_send(sent)
    finish_send(c_send)
    finish_recv(peers(False, pre2, state2, d_s, d_r, pr))
    last = pltpu.make_async_copy(state2, suffix_out, out_sem.at[6])
    last.start()
    finish_send(d_send)
    for one in outs:
        one.wait()
    last.wait()


def gradients(scale, per, k_ref, v_ref, pq_ref, pk_ref, pv_ref, r_ref, dq_ref, dk_ref, dv_ref):
    for h in range(per):
        cols = slice(h * DH, (h + 1) * DH)
        r = r_ref[cols, :]
        dq_ref[:, cols] = scale * pq_ref[:, cols]
        dk_ref[:, cols] = scale * (pk_ref[:, cols] + dot(v_ref[:, cols], r, NT))
        dv_ref[:, cols] = scale * (pv_ref[:, cols] + dot(k_ref[:, cols], r, NN))


def on_device(queries, keys, values, teacher, out_weight, valid):
    rows, width = queries.shape
    heads = width // DH
    model = out_weight.shape[1]
    n_ctx = lax.axis_size("ctx")
    n_x = lax.axis_size("head") // 2
    half = rows // 2
    wide = model // n_x
    part = wide // 2
    tokens = float(rows * n_ctx)
    scale = 1.0 / math.sqrt(DH * rows * n_ctx)
    valid_rows = valid.reshape(rows // DH, DH)
    anywhere = pl.BlockSpec(memory_space=pl.ANY)
    vmem = pl.BlockSpec(memory_space=pltpu.VMEM)
    dma = pltpu.SemaphoreType.DMA
    st = lambda: pltpu.VMEM((heads * DH, DH), BF16)
    whole = jax.ShapeDtypeStruct((rows, width), F32)
    dq, dk, dv, suffix = pl.pallas_call(
        functools.partial(transfer, scale, heads, n_ctx, n_x, tokens),
        name="transfer",
        out_shape=(whole, whole, whole, jax.ShapeDtypeStruct((width, DH), BF16)),
        in_specs=[anywhere] * 5 + [vmem],
        out_specs=(anywhere,) * 4,
        scratch_shapes=[
            pltpu.VMEM((rows, width), BF16),
            pltpu.VMEM((rows, width), BF16),
            pltpu.VMEM((rows, width), BF16),
            pltpu.VMEM((rows, part), BF16),
            pltpu.VMEM((width, model), BF16),
            pltpu.VMEM((rows, width), F32),
            pltpu.VMEM((rows, width), BF16),
            pltpu.VMEM((4, rows, wide), BF16),
            pltpu.VMEM((4, rows, part), BF16),
            pltpu.VMEM((2, half // 2, part), BF16),
            pltpu.VMEM((2, half // 2, part), BF16),
            pltpu.VMEM((rows, part), BF16),
            pltpu.VMEM((rows, part), BF16),
            pltpu.VMEM((n_x, rows, wide), BF16),
            pltpu.VMEM((rows, width), F32),
            pltpu.VMEM((rows, width), BF16),
            pltpu.VMEM((rows, width), F32),
            pltpu.VMEM((rows, width), F32),
            pltpu.VMEM((rows, DH), F32),
            st(), st(), st(), st(), st(), st(), st(), st(),
            pltpu.VMEM((8, 128), F32),
            pltpu.VMEM((8 * n_ctx, 128), F32),
            dma((5,)), dma((7,)),
            dma((n_ctx,)), dma((n_ctx,)), dma((n_ctx,)), dma((n_ctx,)),
            dma((n_ctx,)), dma((n_ctx,)), dma((n_ctx,)), dma((n_ctx,)),
            dma((n_ctx,)), dma((n_ctx,)),
            dma((8,)), dma((8,)), dma((12,)), dma((12,)),
            dma((14,)), dma((14,)), dma((12,)), dma((12,)),
        ],
        compiler_params=pltpu.CompilerParams(
            collective_id=0, has_side_effects=True, vmem_limit_bytes=60 * 1024 * 1024
        ),
    )(queries, keys, values, teacher, out_weight, valid_rows)

    per = 2
    block = pl.BlockSpec((rows, per * DH), lambda i: (0, i))
    square = pl.BlockSpec((per * DH, DH), lambda i: (i, 0))
    return tuple(pl.pallas_call(
        functools.partial(gradients, scale, per),
        name="gradients",
        grid=(heads // per,),
        out_shape=(whole, whole, whole),
        in_specs=[block] * 5 + [square],
        out_specs=(block,) * 3,
    )(keys, values, dq, dk, dv, suffix))


def solution(mesh):
    in_specs = (
        P("ctx", "head"),
        P("ctx", "head"),
        P("ctx", "head"),
        P("ctx", "head"),
        P("head", None),
        P("ctx"),
    )
    out_specs = (P("ctx", "head"), P("ctx", "head"), P("ctx", "head"))
    return jax.shard_map(
        on_device, mesh=mesh, in_specs=in_specs, out_specs=out_specs, check_vma=False
    )
```

time: 109 us -> 99.9 us (0.917)
  Pallas kernels: 106 us -> 98.4 us
    pallas_call x1, Pallas kernels: 11.9 us -> 6.67 us  [on_device(): pl.pallas_call(functools.partial(gradients, scale, per), name='gradients'...]
    pallas_call x1, Pallas kernels: 94.2 us -> 91.7 us  [on_device(): pl.pallas_call(functools.partial(transfer, scale, heads, n_ctx, n_x, toke...]
where the time goes in v2:
time: 99.9 us; the launch traced here: 99 us
  Pallas kernels  98.4 us (98%)
    pallas_call x1, Pallas kernels, on_device(): pl.pallas_call(functools.partial(transfer, scale, heads, n_ctx, n_x, toke...  91.7 us
    pallas_call x1, Pallas kernels, on_device(): pl.pallas_call(functools.partial(gradients, scale, per), name='gradients'...  6.67 us

profile of v2, /device:TPU:1, one launch (start us, length us, event | category | flops | bytes accessed | tf_op | source)
XLA Modules:
  0.0 99.0 jit_solution(4248184183310062012)
XLA Ops:
  0.6 91.7 %transfer.1 = (f32[512,1024]{1,0:T(8,128)}, f32[512,1024]{1,0:T(8,128)}, f32[512,1024]{1,0:T(8,128)}, bf16[1024,128]{1,0:T(8,128)(2,1)}) custom-call(bf16[512,1024]{1,0:T(8,128)(2,1)} %q_hbm.1, bf16[512,1024]{1,0:T(8,128)(2,1)} %k_ref.1, bf16[512,1024]{1,0:T(8,128)(2,1)} %v_ref.1, bf16[512,640]{1,0:T(8,128)(2,1)} %teacher_hbm.1, bf16[1024,5120]{1,0:T(8,128)(2,1)} %w_hbm.1, ...), custom_call_target="tpu_custom_call" | custom-call | tf_op jit(solution)/shard_map/transfer/pallas_call | solution.py:472
  92.4 6.7 %gradients.1 = (f32[512,1024]{1,0:T(8,128)}, f32[512,1024]{1,0:T(8,128)}, f32[512,1024]{1,0:T(8,128)}) custom-call(bf16[512,1024]{1,0:T(8,128)(2,1)} %k_ref.1, bf16[512,1024]{1,0:T(8,128)(2,1)} %v_ref.1, f32[512,1024]{1,0:T(8,128)} %get-tuple-element.7.pq_ref, f32[512,1024]{1,0:T(8,128)} %get-tuple-element.8.pk_ref, f32[512,1024]{1,0:T(8,128)} %get-tuple-element.9.pv_ref, ...), custom_call_target="tpu_custom_call" | custom-call | tf_op jit(solution)/shard_map/gradients/pallas_call | solution.py:516

commit v3 on v2

--- a/solution.py
+++ b/solution.py
@@ -9,6 +9,9 @@
 from jax.sharding import PartitionSpec as P
 
 DH = 128
+UT = True
+UC = True
+UG = 2
 MESH = pl.DeviceIdType.MESH
 F32 = jnp.float32
 BF16 = jnp.bfloat16
@@ -29,10 +32,9 @@
              q_hbm, k_hbm, v_hbm, teacher_hbm, w_hbm, valid_ref,
              dq_out, dk_out, dv_out, suffix_out,
              q, k, v, teacher, w, intra, attn, tp, trecv, relay_p, relay_m, fin_p, fin_m,
-             gath, acc, g, dk, dv, weight, loc, got, pre, state, loc2, got2, pre2, state2, cnt, cnts,
+             gath, acc, g, dq, dk, dv, weight, loc, got, pre, state, loc2, got2, pre2, state2, cnt, cnts,
              in_sem, out_sem, a_s, a_r, b_s, b_r, c_s, c_r, d_s, d_r, n_s, n_r,
              t_s, t_r, x_s, x_r, gp_s, gp_r, gx_s, gx_r):
-    dq = intra
     rows = q.shape[0]
     half = rows // 2
     quarter = rows // 4
@@ -103,7 +105,7 @@
     loads[0].wait()
     loads[1].wait()
 
-    @pl.loop(0, heads)
+    @pl.loop(0, heads, unroll=True)
     def _(h):
         cols = lanes(h * DH, DH)
         loc[head_rows(h), :] = dot(k[:, cols], v[:, cols], TN).astype(BF16)
@@ -136,7 +138,7 @@
     def tri(a, b, mask):
         return jnp.where(mask, dot(a, b, NT), 0.0).astype(BF16)
 
-    @pl.loop(0, heads)
+    @pl.loop(0, heads, unroll=2)
     def _(h):
         cols = lanes(h * DH, DH)
         (k0, k1), (v0, v1), (q0, q1) = both(k, cols), both(v, cols), both(q, cols)
@@ -166,7 +168,7 @@
     def attend(base):
         at = pl.ds(base, half)
 
-        @pl.loop(0, heads)
+        @pl.loop(0, heads, unroll=True)
         def _(h):
             cols = lanes(h * DH, DH)
             carried = dot(q[at, cols], state[head_rows(h), :], NN)
@@ -195,11 +197,24 @@
     targets = [far, near_r, near_l, x]
     t_copies, x_copies = {}, {}
 
+    def first_terms():
+        at = pl.ds(0, half)
+        for mine_too in (0, 1):
+            here = (1 - core if mine_too == 0 else core) * part
+            lo = 0
+            while lo < part:
+                size = min(256, part - lo)
+                tp[0, at, lanes(here + lo, size)] = dot(
+                    attn[at, :], w[:, lanes(far * wide + here + lo, size)], NN).astype(BF16)
+                lo += size
+            if mine_too == 0:
+                t_copies[0, 0] = send(tp.at[0, at, theirs], trecv.at[0, at, :], t_s, t_r, 0, other)
+
     def terms(i, c):
         at = pl.ds(c * half, half)
         base = targets[i] * wide
 
-        @pl.loop(0, wide // 256)
+        @pl.loop(0, wide // 256, unroll=UT)
         def _(n):
             tp[i, at, lanes(n * 256, 256)] = dot(attn[at, :], w[:, lanes(base + n * 256, 256)], NN).astype(BF16)
 
@@ -310,7 +325,7 @@
     def contract(block, c, lo=0, size=wide, fresh=False):
         at = pl.ds(c * half, half)
 
-        @pl.loop(0, heads * DH // 256)
+        @pl.loop(0, heads * DH // 256, unroll=UC)
         def _(n):
             cols = lanes(n * 256, 256)
             new = dot(
@@ -341,7 +356,7 @@
         contract(far, c, (1 - core) * part, part)
 
     attend(0)
-    terms(0, 0)
+    first_terms()
     terms(1, 0)
     far_out(0)
     terms(2, 0)
@@ -368,7 +383,7 @@
     far_in(0)
     contract_far(0)
 
-    @pl.loop(0, heads)
+    @pl.loop(0, heads, unroll=True)
     def _(h):
         cols = lanes(h * DH, DH)
         g_h = acc[0:half, cols].astype(BF16)
@@ -376,21 +391,12 @@
         acc[0:DH, cols] = dot(q[0:half, cols], g_h, TN)
 
     near_first(1)
-
-    @pl.loop(0, heads)
-    def _(h):
-        cols = lanes(h * DH, DH)
-        k0, v0, q0, g0 = k[0:half, cols], v[0:half, cols], q[0:half, cols], g[0:half, cols]
-        dq[0:half, cols] = dot(tri(g0, v0, lower), k0, NN) + dot(g0, state[head_rows(h), :], NT)
-        dk[0:half, cols] = dot(tri(v0, g0, upper), q0, NN)
-        dv[0:half, cols] = dot(tri(k0, q0, upper), g0, NN)
-
     near_second(1)
     contract_near(1)
     far_in(1)
     contract_far(1)
 
-    @pl.loop(0, heads)
+    @pl.loop(0, heads, unroll=True)
     def _(h):
         cols = lanes(h * DH, DH)
         g_h = acc[half:rows, cols].astype(BF16)
@@ -403,20 +409,20 @@
 
     outs = []
 
-    def second_half(lo, hi):
-        @pl.loop(lo, hi)
+    def block_gradients(lo, hi):
+        @pl.loop(lo, hi, unroll=UG)
         def _(h):
             cols = lanes(h * DH, DH)
-            (k0, k1), (v0, v1), (q0, q1) = both(k, cols), both(v, cols), both(q, cols)
-            g1 = g[half:rows, cols]
+            (k0, k1), (v0, v1), (q0, q1), (g0, g1) = both(k, cols), both(v, cols), both(q, cols), both(g, cols)
+            p = state[head_rows(h), :]
+            dq[0:half, cols] = (dot(tri(g0, v0, lower), k0, NN) + dot(g0, p, NT)).astype(BF16)
             dq[half:rows, cols] = (
-                dot(full(g1, v0), k0, NN) + dot(tri(g1, v1, lower), k1, NN)
-                + dot(g1, state[head_rows(h), :], NT)
-            )
-            dk[0:half, cols] += dot(full(v0, g1), q1, NN)
-            dk[half:rows, cols] = dot(tri(v1, g1, upper), q1, NN)
-            dv[0:half, cols] += dot(full(k0, q1), g1, NN)
-            dv[half:rows, cols] = dot(tri(k1, q1, upper), g1, NN)
+                dot(full(g1, v0), k0, NN) + dot(tri(g1, v1, lower), k1, NN) + dot(g1, p, NT)
+            ).astype(BF16)
+            dk[0:half, cols] = (dot(tri(v0, g0, upper), q0, NN) + dot(full(v0, g1), q1, NN)).astype(BF16)
+            dk[half:rows, cols] = dot(tri(v1, g1, upper), q1, NN).astype(BF16)
+            dv[0:half, cols] = (dot(tri(k0, q0, upper), g0, NN) + dot(full(k0, q1), g1, NN)).astype(BF16)
+            dv[half:rows, cols] = dot(tri(k1, q1, upper), g1, NN).astype(BF16)
 
         cols = pl.ds(lo * DH, (hi - lo) * DH)
         for src, dst in ((dq, dq_out), (dk, dk_out), (dv, dv_out)):
@@ -424,13 +430,13 @@
             copy.start()
             outs.append(copy)
 
-    second_half(0, heads // 2)
+    block_gradients(0, heads // 2)
     finish_recv(peers(False, loc2, got2, c_s, c_r, pr))
     scan(got2, pre2, True)
     d_send = peers(True, pre2, state2, d_s, d_r, pr)
     start(d_send)
     state2[mine(pr), :] = pre2[mine(pr), :]
-    second_half(heads // 2, heads)
+    block_gradients(heads // 2, heads)
     finish_send(b_send)
     finish_send(sent)
     finish_send(c_send)
@@ -443,13 +449,13 @@
     last.wait()
 
 
-def gradients(scale, per, k_ref, v_ref, pq_ref, pk_ref, pv_ref, r_ref, dq_ref, dk_ref, dv_ref):
-    for h in range(per):
+def gradients(scale, k_ref, v_ref, pq_ref, pk_ref, pv_ref, r_ref, dq_ref, dk_ref, dv_ref):
+    for h in range(k_ref.shape[1] // DH):
         cols = slice(h * DH, (h + 1) * DH)
         r = r_ref[cols, :]
-        dq_ref[:, cols] = scale * pq_ref[:, cols]
-        dk_ref[:, cols] = scale * (pk_ref[:, cols] + dot(v_ref[:, cols], r, NT))
-        dv_ref[:, cols] = scale * (pv_ref[:, cols] + dot(k_ref[:, cols], r, NN))
+        dq_ref[:, cols] = scale * pq_ref[:, cols].astype(F32)
+        dk_ref[:, cols] = scale * (pk_ref[:, cols].astype(F32) + dot(v_ref[:, cols], r, NT))
+        dv_ref[:, cols] = scale * (pv_ref[:, cols].astype(F32) + dot(k_ref[:, cols], r, NN))
 
 
 def on_device(queries, keys, values, teacher, out_weight, valid):
@@ -468,7 +474,7 @@
     vmem = pl.BlockSpec(memory_space=pltpu.VMEM)
     dma = pltpu.SemaphoreType.DMA
     st = lambda: pltpu.VMEM((heads * DH, DH), BF16)
-    whole = jax.ShapeDtypeStruct((rows, width), F32)
+    whole = jax.ShapeDtypeStruct((rows, width), BF16)
     dq, dk, dv, suffix = pl.pallas_call(
         functools.partial(transfer, scale, heads, n_ctx, n_x, tokens),
         name="transfer",
@@ -492,8 +498,9 @@
             pltpu.VMEM((n_x, rows, wide), BF16),
             pltpu.VMEM((rows, width), F32),
             pltpu.VMEM((rows, width), BF16),
-            pltpu.VMEM((rows, width), F32),
-            pltpu.VMEM((rows, width), F32),
+            pltpu.VMEM((rows, width), BF16),
+            pltpu.VMEM((rows, width), BF16),
+            pltpu.VMEM((rows, width), BF16),
             pltpu.VMEM((rows, DH), F32),
             st(), st(), st(), st(), st(), st(), st(), st(),
             pltpu.VMEM((8, 128), F32),
@@ -510,14 +517,14 @@
         ),
     )(queries, keys, values, teacher, out_weight, valid_rows)
 
-    per = 2
+    per = 4
     block = pl.BlockSpec((rows, per * DH), lambda i: (0, i))
     square = pl.BlockSpec((per * DH, DH), lambda i: (i, 0))
     return tuple(pl.pallas_call(
-        functools.partial(gradients, scale, per),
+        functools.partial(gradients, scale),
         name="gradients",
         grid=(heads // per,),
-        out_shape=(whole, whole, whole),
+        out_shape=(jax.ShapeDtypeStruct((rows, width), F32),) * 3,
         in_specs=[block] * 5 + [square],
         out_specs=(block,) * 3,
     )(keys, values, dq, dk, dv, suffix))

time: 99.9 us -> 90.5 us (0.906)
  Pallas kernels: 98.4 us -> 89.4 us
    pallas_call x1, Pallas kernels: 91.7 us -> 84.4 us  [on_device(): pl.pallas_call(functools.partial(transfer, scale, heads, n_ctx, n_x, toke...]
    pallas_call x1, Pallas kernels: 6.67 us -> 4.94 us  [on_device(): pl.pallas_call(functools.partial(gradients, scale), name='gradients', gri...]
where the time goes in v3:
time: 90.5 us; the launch traced here: 90 us
  Pallas kernels  89.4 us (99%)
    pallas_call x1, Pallas kernels, on_device(): pl.pallas_call(functools.partial(transfer, scale, heads, n_ctx, n_x, toke...  84.4 us
    pallas_call x1, Pallas kernels, on_device(): pl.pallas_call(functools.partial(gradients, scale), name='gradients', gri...  4.94 us

profile of v3, /device:TPU:1, one launch (start us, length us, event | category | flops | bytes accessed | tf_op | source)
XLA Modules:
  0.0 90.0 jit_solution(6221969881857233850)
XLA Ops:
  0.6 84.4 %transfer.1 = (bf16[512,1024]{1,0:T(8,128)(2,1)}, bf16[512,1024]{1,0:T(8,128)(2,1)}, bf16[512,1024]{1,0:T(8,128)(2,1)}, bf16[1024,128]{1,0:T(8,128)(2,1)}) custom-call(bf16[512,1024]{1,0:T(8,128)(2,1)} %q_hbm.1, bf16[512,1024]{1,0:T(8,128)(2,1)} %k_ref.1, bf16[512,1024]{1,0:T(8,128)(2,1)} %v_ref.1, bf16[512,640]{1,0:T(8,128)(2,1)} %teacher_hbm.1, ...), custom_call_target="tpu_custom_call" | custom-call | tf_op jit(solution)/shard_map/transfer/pallas_call | solution.py:478
  85.1 4.9 %gradients.1 = (f32[512,1024]{1,0:T(8,128)}, f32[512,1024]{1,0:T(8,128)}, f32[512,1024]{1,0:T(8,128)}) custom-call(bf16[512,1024]{1,0:T(8,128)(2,1)} %k_ref.1, bf16[512,1024]{1,0:T(8,128)(2,1)} %v_ref.1, bf16[512,1024]{1,0:T(8,128)(2,1)} %get-tuple-element.7.pq_ref, bf16[512,1024]{1,0:T(8,128)(2,1)} %get-tuple-element.8.pk_ref, ...), custom_call_target="tpu_custom_call" | custom-call | tf_op jit(solution)/shard_map/gradients/pallas_call | solution.py:523

commit v4 on v3

--- a/solution.py
+++ b/solution.py
@@ -12,6 +12,7 @@
 UT = True
 UC = True
 UG = 2
+LIMIT = 54
 MESH = pl.DeviceIdType.MESH
 F32 = jnp.float32
 BF16 = jnp.bfloat16
@@ -30,10 +31,10 @@
 
 def transfer(scale, heads, n_ctx, n_x, tokens,
              q_hbm, k_hbm, v_hbm, teacher_hbm, w_hbm, valid_ref,
-             dq_out, dk_out, dv_out, suffix_out,
-             q, k, v, teacher, w, intra, attn, tp, trecv, relay_p, relay_m, fin_p, fin_m,
-             gath, acc, g, dq, dk, dv, weight, loc, got, pre, state, loc2, got2, pre2, state2, cnt, cnts,
-             in_sem, out_sem, a_s, a_r, b_s, b_r, c_s, c_r, d_s, d_r, n_s, n_r,
+             k, v, dq, dk, dv, suffix,
+             q, teacher, w, intra, attn, tp, trecv, relay_p, relay_m, fin_p, fin_m,
+             gath, acc, g, weight, loc, got, pre, state, loc2, got2, pre2, state2, cnt, cnts,
+             in_sem, a_s, a_r, b_s, b_r, c_s, c_r, d_s, d_r, n_s, n_r,
              t_s, t_r, x_s, x_r, gp_s, gp_r, gx_s, gx_r):
     rows = q.shape[0]
     half = rows // 2
@@ -61,10 +62,19 @@
     for one in loads[:3]:
         one.start()
 
+    n_y = math.isqrt(n_ctx) if math.isqrt(n_ctx) ** 2 == n_ctx else n_ctx
+    n_z = n_ctx // n_y
+    offsets = sorted(
+        ((i, j) for i in range(n_z) for j in range(n_y) if i or j),
+        key=lambda o: -min(o[0], n_z - o[0]) - min(o[1], n_y - o[1]),
+    )
+
     def peers(sending, src, dst, ssem, rsem, piece):
         out = []
-        for d in range(1, n_ctx):
-            peer = (me_c + d) % n_ctx if sending else (me_c + n_ctx - d) % n_ctx
+        for d, (oz, oy) in enumerate(offsets):
+            if not sending:
+                oz, oy = n_z - oz, n_y - oy
+            peer = ((me_c // n_y + oz) % n_z) * n_y + (me_c % n_y + oy) % n_y
             place = me_c if sending else peer
             out.append(pltpu.make_async_remote_copy(
                 src_ref=src.at[pl.ds(pl.multiple_of(peer * piece, piece), piece)] if src is not cnt else src,
@@ -407,28 +417,20 @@
     start(c_send)
     got2[mine(pr), :] = loc2[mine(pr), :]
 
-    outs = []
-
     def block_gradients(lo, hi):
         @pl.loop(lo, hi, unroll=UG)
         def _(h):
             cols = lanes(h * DH, DH)
             (k0, k1), (v0, v1), (q0, q1), (g0, g1) = both(k, cols), both(v, cols), both(q, cols), both(g, cols)
             p = state[head_rows(h), :]
-            dq[0:half, cols] = (dot(tri(g0, v0, lower), k0, NN) + dot(g0, p, NT)).astype(BF16)
-            dq[half:rows, cols] = (
+            dq[0:half, cols] = scale * (dot(tri(g0, v0, lower), k0, NN) + dot(g0, p, NT))
+            dq[half:rows, cols] = scale * (
                 dot(full(g1, v0), k0, NN) + dot(tri(g1, v1, lower), k1, NN) + dot(g1, p, NT)
-            ).astype(BF16)
-            dk[0:half, cols] = (dot(tri(v0, g0, upper), q0, NN) + dot(full(v0, g1), q1, NN)).astype(BF16)
-            dk[half:rows, cols] = dot(tri(v1, g1, upper), q1, NN).astype(BF16)
-            dv[0:half, cols] = (dot(tri(k0, q0, upper), g0, NN) + dot(full(k0, q1), g1, NN)).astype(BF16)
-            dv[half:rows, cols] = dot(tri(k1, q1, upper), g1, NN).astype(BF16)
-
-        cols = pl.ds(lo * DH, (hi - lo) * DH)
-        for src, dst in ((dq, dq_out), (dk, dk_out), (dv, dv_out)):
-            copy = pltpu.make_async_copy(src.at[:, cols], dst.at[:, cols], out_sem.at[len(outs)])
-            copy.start()
-            outs.append(copy)
+            )
+            dk[0:half, cols] = dot(tri(v0, g0, upper), q0, NN) + dot(full(v0, g1), q1, NN)
+            dk[half:rows, cols] = dot(tri(v1, g1, upper), q1, NN)
+            dv[0:half, cols] = dot(tri(k0, q0, upper), g0, NN) + dot(full(k0, q1), g1, NN)
+            dv[half:rows, cols] = dot(tri(k1, q1, upper), g1, NN)
 
     block_gradients(0, heads // 2)
     finish_recv(peers(False, loc2, got2, c_s, c_r, pr))
@@ -441,21 +443,28 @@
     finish_send(sent)
     finish_send(c_send)
     finish_recv(peers(False, pre2, state2, d_s, d_r, pr))
-    last = pltpu.make_async_copy(state2, suffix_out, out_sem.at[6])
-    last.start()
+    suffix[...] = state2[...]
     finish_send(d_send)
-    for one in outs:
-        one.wait()
-    last.wait()
-
-
-def gradients(scale, k_ref, v_ref, pq_ref, pk_ref, pv_ref, r_ref, dq_ref, dk_ref, dv_ref):
-    for h in range(k_ref.shape[1] // DH):
-        cols = slice(h * DH, (h + 1) * DH)
-        r = r_ref[cols, :]
-        dq_ref[:, cols] = scale * pq_ref[:, cols].astype(F32)
-        dk_ref[:, cols] = scale * (pk_ref[:, cols].astype(F32) + dot(v_ref[:, cols], r, NT))
-        dv_ref[:, cols] = scale * (pv_ref[:, cols].astype(F32) + dot(k_ref[:, cols], r, NN))
+
+
+def gradients(scale, k, v, dq, pk, pv, suffix, dq_out, dk_out, dv_out, dk, dv, sems):
+    heads = k.shape[1] // DH
+    step = 2
+    copies = [pltpu.make_async_copy(dq, dq_out, sems.at[heads])]
+    copies[0].start()
+    for group in range(heads // step):
+        for h in range(group * step, (group + 1) * step):
+            cols = slice(h * DH, (h + 1) * DH)
+            r = suffix[cols, :]
+            dk[:, cols] = scale * (pk[:, cols] + dot(v[:, cols], r, NT))
+            dv[:, cols] = scale * (pv[:, cols] + dot(k[:, cols], r, NN))
+        span = pl.ds(group * step * DH, step * DH)
+        for n, (src, dst) in enumerate(((dk, dk_out), (dv, dv_out))):
+            copy = pltpu.make_async_copy(src.at[:, span], dst.at[:, span], sems.at[2 * group + n])
+            copy.start()
+            copies.append(copy)
+    for copy in copies:
+        copy.wait()
 
 
 def on_device(queries, keys, values, teacher, out_weight, valid):
@@ -474,16 +483,14 @@
     vmem = pl.BlockSpec(memory_space=pltpu.VMEM)
     dma = pltpu.SemaphoreType.DMA
     st = lambda: pltpu.VMEM((heads * DH, DH), BF16)
-    whole = jax.ShapeDtypeStruct((rows, width), BF16)
-    dq, dk, dv, suffix = pl.pallas_call(
+    kept = pltpu.VMEM((rows, width), BF16)
+    passed = pl.pallas_call(
         functools.partial(transfer, scale, heads, n_ctx, n_x, tokens),
         name="transfer",
-        out_shape=(whole, whole, whole, jax.ShapeDtypeStruct((width, DH), BF16)),
+        out_shape=(kept,) * 2 + (pltpu.VMEM((rows, width), F32),) * 3 + (pltpu.VMEM((width, DH), BF16),),
         in_specs=[anywhere] * 5 + [vmem],
-        out_specs=(anywhere,) * 4,
+        out_specs=(vmem,) * 6,
         scratch_shapes=[
-            pltpu.VMEM((rows, width), BF16),
-            pltpu.VMEM((rows, width), BF16),
             pltpu.VMEM((rows, width), BF16),
             pltpu.VMEM((rows, part), BF16),
             pltpu.VMEM((width, model), BF16),
@@ -498,14 +505,11 @@
             pltpu.VMEM((n_x, rows, wide), BF16),
             pltpu.VMEM((rows, width), F32),
             pltpu.VMEM((rows, width), BF16),
-            pltpu.VMEM((rows, width), BF16),
-            pltpu.VMEM((rows, width), BF16),
-            pltpu.VMEM((rows, width), BF16),
             pltpu.VMEM((rows, DH), F32),
             st(), st(), st(), st(), st(), st(), st(), st(),
             pltpu.VMEM((8, 128), F32),
             pltpu.VMEM((8 * n_ctx, 128), F32),
-            dma((5,)), dma((7,)),
+            dma((5,)),
             dma((n_ctx,)), dma((n_ctx,)), dma((n_ctx,)), dma((n_ctx,)),
             dma((n_ctx,)), dma((n_ctx,)), dma((n_ctx,)), dma((n_ctx,)),
             dma((n_ctx,)), dma((n_ctx,)),
@@ -513,21 +517,19 @@
             dma((14,)), dma((14,)), dma((12,)), dma((12,)),
         ],
         compiler_params=pltpu.CompilerParams(
-            collective_id=0, has_side_effects=True, vmem_limit_bytes=60 * 1024 * 1024
+            collective_id=0, has_side_effects=True, vmem_limit_bytes=LIMIT * 1024 * 1024
         ),
     )(queries, keys, values, teacher, out_weight, valid_rows)
 
-    per = 4
-    block = pl.BlockSpec((rows, per * DH), lambda i: (0, i))
-    square = pl.BlockSpec((per * DH, DH), lambda i: (i, 0))
     return tuple(pl.pallas_call(
         functools.partial(gradients, scale),
         name="gradients",
-        grid=(heads // per,),
         out_shape=(jax.ShapeDtypeStruct((rows, width), F32),) * 3,
-        in_specs=[block] * 5 + [square],
-        out_specs=(block,) * 3,
-    )(keys, values, dq, dk, dv, suffix))
+        in_specs=[vmem] * 6,
+        out_specs=(anywhere,) * 3,
+        scratch_shapes=[pltpu.VMEM((rows, width), F32)] * 2 + [dma((heads + 1,))],
+        compiler_params=pltpu.CompilerParams(vmem_limit_bytes=16 * 1024 * 1024),
+    )(*passed))
 
 
 def solution(mesh):

time: 90.5 us -> 87 us (0.961)
  Pallas kernels: 89.4 us -> 86 us
    pallas_call x1, Pallas kernels: 4.94 us -> 2.73 us  [on_device(): pl.pallas_call(functools.partial(gradients, scale), name='gradients', out...]
    pallas_call x1, Pallas kernels: 84.4 us -> 83.3 us  [on_device(): pl.pallas_call(functools.partial(transfer, scale, heads, n_ctx, n_x, toke...]
where the time goes in v4:
time: 87 us; the launch traced here: 86.8 us
  Pallas kernels  86 us (99%)
    pallas_call x1, Pallas kernels, on_device(): pl.pallas_call(functools.partial(transfer, scale, heads, n_ctx, n_x, toke...  83.3 us
    pallas_call x1, Pallas kernels, on_device(): pl.pallas_call(functools.partial(gradients, scale), name='gradients', out...  2.73 us

profile of v4, /device:TPU:1, one launch (start us, length us, event | category | flops | bytes accessed | tf_op | source)
XLA Modules:
  0.0 86.8 jit_solution(15481810272546315954)
XLA Ops:
  0.6 83.3 %transfer.1 = (bf16[512,1024]{1,0:T(8,128)(2,1)S(1)}, bf16[512,1024]{1,0:T(8,128)(2,1)S(1)}, f32[512,1024]{1,0:T(8,128)S(1)}, f32[512,1024]{1,0:T(8,128)S(1)}, f...) custom-call(bf16[512,1024]{1,0:T(8,128)(2,1)} %q_hbm.1, bf16[512,1024]{1,0:T(8,128)(2,1)} %k_hbm.1, ...), custom_call_target="tpu_custom_call" | custom-call | tf_op jit(solution)/shard_map/transfer/pallas_call | solution.py:487
  83.9 2.7 %gradients.1 = (f32[512,1024]{1,0:T(8,128)}, f32[512,1024]{1,0:T(8,128)}, f32[512,1024]{1,0:T(8,128)}) custom-call(bf16[512,1024]{1,0:T(8,128)(2,1)S(1)} %get-tuple-element.9.k, bf16[512,1024]{1,0:T(8,128)(2,1)S(1)} %get-tuple-element.10.v, f32[512,1024]{1,0:T(8,128)S(1)} %get-tuple-element.11.dq, f32[512,1024]{1,0:T(8,128)S(1)} %get-tuple-element.12.pk, ...), custom_call_target="tpu_custom_call" | custom-call | tf_op jit(solution)/shard_map/gradients/pallas_call | solution.py:524

commit v5 on v4

--- a/solution.py
+++ b/solution.py
@@ -122,14 +122,11 @@
 
     loads[3].start()
     loads[4].start()
-    flags = valid_ref[...].astype(F32)
-    cnt[...] = jnp.zeros_like(cnt) + jnp.sum(flags)
+    cnt[...] = jnp.zeros_like(cnt) + jnp.sum(valid_ref[...].astype(F32))
     pl.semaphore_wait(barrier, n_ctx - 1 + 3)
 
     a_send = peers(True, loc, got, a_s, a_r, pr)
-    n_send = peers(True, cnt, cnts, n_s, n_r, 8)
     start(a_send)
-    start(n_send)
     got[mine(pr), :] = loc[mine(pr), :]
     cnts[mine(8), :] = cnt[...]
 
@@ -159,24 +156,27 @@
     scan(got, pre, False)
     b_send = peers(True, pre, state, b_s, b_r, pr)
     start(b_send)
+    n_send = peers(True, cnt, cnts, n_s, n_r, 8)
+    start(n_send)
     state[mine(pr), :] = pre[mine(pr), :]
     finish_send(a_send)
-    finish_send(n_send)
-    finish_recv(peers(False, cnt, cnts, n_s, n_r, 8))
-    count = cnts[0:8, :]
-    for j in range(1, n_ctx):
-        count = count + cnts[j * 8 : j * 8 + 8, :]
-    factor = (tokens / count)[0:1, :]
-    diagonal = row[0:DH, 0:DH] == col[0:DH, 0:DH]
-    for j in range(rows // DH):
-        column = jnp.sum(jnp.where(diagonal, flags[j : j + 1, :], 0.0), axis=1, keepdims=True)
-        weight[j * DH : (j + 1) * DH, :] = column * factor
     loads[3].wait()
     loads[4].wait()
     finish_recv(peers(False, pre, state, b_s, b_r, pr))
 
-    def attend(base):
-        at = pl.ds(base, half)
+    def weigh():
+        finish_recv(peers(False, cnt, cnts, n_s, n_r, 8))
+        count = cnts[0:8, :]
+        for j in range(1, n_ctx):
+            count = count + cnts[j * 8 : j * 8 + 8, :]
+        factor = (tokens / count)[0:1, :]
+        diagonal = row[0:DH, 0:DH] == col[0:DH, 0:DH]
+        for j in range(rows // DH):
+            column = jnp.sum(jnp.where(diagonal, valid_ref[j : j + 1, :].astype(F32), 0.0), axis=1, keepdims=True)
+            weight[j * DH : (j + 1) * DH, :] = column * factor
+
+    def attend(base, size):
+        at = pl.ds(base, size)
 
         @pl.loop(0, heads, unroll=True)
         def _(h):
@@ -207,18 +207,26 @@
     targets = [far, near_r, near_l, x]
     t_copies, x_copies = {}, {}
 
+    def some_terms(at, here):
+        lo = 0
+        while lo < part:
+            size = min(256, part - lo)
+            tp[0, at, lanes(here + lo, size)] = dot(
+                attn[at, :], w[:, lanes(far * wide + here + lo, size)], NN).astype(BF16)
+            lo += size
+
     def first_terms():
-        at = pl.ds(0, half)
-        for mine_too in (0, 1):
-            here = (1 - core if mine_too == 0 else core) * part
-            lo = 0
-            while lo < part:
-                size = min(256, part - lo)
-                tp[0, at, lanes(here + lo, size)] = dot(
-                    attn[at, :], w[:, lanes(far * wide + here + lo, size)], NN).astype(BF16)
-                lo += size
-            if mine_too == 0:
-                t_copies[0, 0] = send(tp.at[0, at, theirs], trecv.at[0, at, :], t_s, t_r, 0, other)
+        parts = quarters(0)
+        copies = []
+        for n, at in enumerate(parts):
+            attend(n * quarter, quarter)
+            some_terms(at, (1 - core) * part)
+            copies.append(send(tp.at[0, at, theirs], trecv.at[0, at, :], t_s, t_r, (0, 8)[n], other))
+        some_terms(pl.ds(0, half), core * part)
+        for n, (at, relay, device) in enumerate(zip(parts, (relay_p, relay_m), (right, left))):
+            copies[n].wait_recv()
+            add_rows(0, n * quarter, quarter)
+            send_x(n, 0, tp.at[0, at, own], relay.at[0], device)
 
     def terms(i, c):
         at = pl.ds(c * half, half)
@@ -232,14 +240,16 @@
 
     def add_chip(i, c):
         t_copies[i, c].wait_recv()
-
-        @pl.loop(0, half // step_rows)
+        add_rows(i, c * half, half)
+
+    def add_rows(i, base, size):
+        @pl.loop(0, size // step_rows, unroll=True)
         def _(r):
-            at = pl.ds(pl.multiple_of(c * half + r * step_rows, step_rows), step_rows)
+            at = pl.ds(pl.multiple_of(base + r * step_rows, step_rows), step_rows)
             tp[i, at, own] = (tp[i, at, own].astype(F32) + trecv[i, at, :].astype(F32)).astype(BF16)
 
     def add_relay(i, rel, c, base):
-        @pl.loop(0, quarter // step_rows)
+        @pl.loop(0, quarter // step_rows, unroll=True)
         def _(r):
             off = pl.multiple_of(r * step_rows, step_rows)
             at = pl.ds(base + off, step_rows)
@@ -294,7 +304,7 @@
         for n in (2, 3, 4, 5):
             x_copies[n, c].wait_recv()
 
-        @pl.loop(0, half // step_rows)
+        @pl.loop(0, half // step_rows, unroll=True)
         def _(r):
             at = pl.ds(pl.multiple_of(c * half + r * step_rows, step_rows), step_rows)
             pred = tp[3, at, own].astype(F32) + trecv[3, at, :].astype(F32)
@@ -365,15 +375,13 @@
         from_other(6, c, far, qb)
         contract(far, c, (1 - core) * part, part)
 
-    attend(0)
     first_terms()
     terms(1, 0)
-    far_out(0)
     terms(2, 0)
     right_out(0)
     terms(3, 0)
     left_out(0)
-    attend(half)
+    attend(half, half)
     terms(0, 1)
     relayed(0)
     terms(1, 1)
@@ -382,6 +390,7 @@
     right_out(1)
     terms(3, 1)
     left_out(1)
+    weigh()
     error(0)
     relayed(1)
     contract_own(0)
@@ -440,6 +449,7 @@
     state2[mine(pr), :] = pre2[mine(pr), :]
     block_gradients(heads // 2, heads)
     finish_send(b_send)
+    finish_send(n_send)
     finish_send(sent)
     finish_send(c_send)
     finish_recv(peers(False, pre2, state2, d_s, d_r, pr))
@@ -513,7 +523,7 @@
             dma((n_ctx,)), dma((n_ctx,)), dma((n_ctx,)), dma((n_ctx,)),
             dma((n_ctx,)), dma((n_ctx,)), dma((n_ctx,)), dma((n_ctx,)),
             dma((n_ctx,)), dma((n_ctx,)),
-            dma((8,)), dma((8,)), dma((12,)), dma((12,)),
+            dma((9,)), dma((9,)), dma((12,)), dma((12,)),
             dma((14,)), dma((14,)), dma((12,)), dma((12,)),
         ],
         compiler_params=pltpu.CompilerParams(

time: 87 us -> 86 us (0.989)
  Pallas kernels: 86 us -> 85 us
    pallas_call x1, Pallas kernels: 83.3 us -> 82.3 us  [on_device(): pl.pallas_call(functools.partial(transfer, scale, heads, n_ctx, n_x, toke...]
where the time goes in v5:
time: 86 us; the launch traced here: 85.8 us
  Pallas kernels  85 us (99%)
    pallas_call x1, Pallas kernels, on_device(): pl.pallas_call(functools.partial(transfer, scale, heads, n_ctx, n_x, toke...  82.3 us
    pallas_call x1, Pallas kernels, on_device(): pl.pallas_call(functools.partial(gradients, scale), name='gradients', out...  2.73 us

profile of v5, /device:TPU:1, one launch (start us, length us, event | category | flops | bytes accessed | tf_op | source)
XLA Modules:
  0.0 85.8 jit_solution(8924746214476840989)
XLA Ops:
  0.6 82.3 %transfer.1 = (bf16[512,1024]{1,0:T(8,128)(2,1)S(1)}, bf16[512,1024]{1,0:T(8,128)(2,1)S(1)}, f32[512,1024]{1,0:T(8,128)S(1)}, f32[512,1024]{1,0:T(8,128)S(1)}, f...) custom-call(bf16[512,1024]{1,0:T(8,128)(2,1)} %q_hbm.1, bf16[512,1024]{1,0:T(8,128)(2,1)} %k_hbm.1, ...), custom_call_target="tpu_custom_call" | custom-call | tf_op jit(solution)/shard_map/transfer/pallas_call | solution.py:497
  83.0 2.7 %gradients.1 = (f32[512,1024]{1,0:T(8,128)}, f32[512,1024]{1,0:T(8,128)}, f32[512,1024]{1,0:T(8,128)}) custom-call(bf16[512,1024]{1,0:T(8,128)(2,1)S(1)} %get-tuple-element.9.k, bf16[512,1024]{1,0:T(8,128)(2,1)S(1)} %get-tuple-element.10.v, f32[512,1024]{1,0:T(8,128)S(1)} %get-tuple-element.11.dq, f32[512,1024]{1,0:T(8,128)S(1)} %get-tuple-element.12.pk, ...), custom_call_target="tpu_custom_call" | custom-call | tf_op jit(solution)/shard_map/gradients/pallas_call | solution.py:534

commit v6 on v5

--- a/solution.py
+++ b/solution.py
@@ -12,6 +12,7 @@
 UT = True
 UC = True
 UG = 2
+CHUNKS = (320, 192)
 LIMIT = 54
 MESH = pl.DeviceIdType.MESH
 F32 = jnp.float32
@@ -38,7 +39,7 @@
              t_s, t_r, x_s, x_r, gp_s, gp_r, gx_s, gx_r):
     rows = q.shape[0]
     half = rows // 2
-    quarter = rows // 4
+    starts = (0, CHUNKS[0])
     wide = w.shape[1] // n_x
     part = wide // 2
     me_c = lax.axis_index("ctx")
@@ -92,13 +93,35 @@
     def head_rows(h):
         return pl.ds(pl.multiple_of(h * DH, DH), DH)
 
-    def scan(got_ref, pre_ref, backward):
+    def to_peer(j, src, dst, ssem, rsem):
+        return pltpu.make_async_remote_copy(
+            src_ref=src.at[j * pr : (j + 1) * pr], dst_ref=dst.at[mine(pr)],
+            send_sem=ssem.at[j], recv_sem=rsem.at[me_c],
+            device_id=(j, me_h), device_id_type=MESH)
+
+    def scan(loc_ref, got_ref, pre_ref, state_ref, ssem, rsem, ssem2, rsem2, backward):
         total = jnp.zeros((pr, DH), F32)
         order = range(n_ctx - 1, -1, -1) if backward else range(n_ctx)
         for j in order:
             block = slice(j * pr, (j + 1) * pr)
             pre_ref[block, :] = total.astype(BF16)
+
+            @pl.when(me_c != j)
+            def _():
+                to_peer(j, pre_ref, state_ref, ssem2, rsem2).start()
+                pltpu.make_async_remote_copy(
+                    src_ref=loc_ref.at[block], dst_ref=got_ref.at[block],
+                    send_sem=ssem.at[0], recv_sem=rsem.at[j],
+                    device_id=(j, me_h), device_id_type=MESH).wait_recv()
+
             total = total + got_ref[block, :].astype(F32)
+        state_ref[mine(pr), :] = pre_ref[mine(pr), :]
+
+    def finish_scan(pre_ref, state_ref, ssem2, rsem2):
+        for j in range(n_ctx):
+            @pl.when(me_c != j)
+            def _():
+                to_peer(j, pre_ref, state_ref, ssem2, rsem2).wait_send()
 
     def start(copies):
         for one in copies:
@@ -152,13 +175,9 @@
         intra[0:half, cols] = dot(tri(q0, k0, lower), v0, NN)
         intra[half:rows, cols] = dot(full(q1, k0), v0, NN) + dot(tri(q1, k1, lower), v1, NN)
 
-    finish_recv(peers(False, loc, got, a_s, a_r, pr))
-    scan(got, pre, False)
-    b_send = peers(True, pre, state, b_s, b_r, pr)
-    start(b_send)
+    scan(loc, got, pre, state, a_s, a_r, b_s, b_r, False)
     n_send = peers(True, cnt, cnts, n_s, n_r, 8)
     start(n_send)
-    state[mine(pr), :] = pre[mine(pr), :]
     finish_send(a_send)
     loads[3].wait()
     loads[4].wait()
@@ -191,7 +210,7 @@
 
     own = lanes(core * part, part)
     theirs = lanes((1 - core) * part, part)
-    step_rows = 64
+    step_rows = 32
     sent = []
 
     def send(src, dst, ssem, rsem, n, device):
@@ -201,7 +220,11 @@
         return copy
 
     def quarters(c):
-        return pl.ds(2 * c * quarter, quarter), pl.ds((2 * c + 1) * quarter, quarter)
+        size = CHUNKS[c] // 2
+        return pl.ds(starts[c], size), pl.ds(starts[c] + size, size)
+
+    def chunk(c):
+        return pl.ds(starts[c], CHUNKS[c])
 
     near_r, near_l, far = (x + 1) % n_x, (x + n_x - 1) % n_x, (x + 2) % n_x
     targets = [far, near_r, near_l, x]
@@ -219,17 +242,17 @@
         parts = quarters(0)
         copies = []
         for n, at in enumerate(parts):
-            attend(n * quarter, quarter)
+            attend(n * CHUNKS[0] // 2, CHUNKS[0] // 2)
             some_terms(at, (1 - core) * part)
             copies.append(send(tp.at[0, at, theirs], trecv.at[0, at, :], t_s, t_r, (0, 8)[n], other))
-        some_terms(pl.ds(0, half), core * part)
+        some_terms(chunk(0), core * part)
         for n, (at, relay, device) in enumerate(zip(parts, (relay_p, relay_m), (right, left))):
             copies[n].wait_recv()
-            add_rows(0, n * quarter, quarter)
-            send_x(n, 0, tp.at[0, at, own], relay.at[0], device)
+            add_rows(0, n * CHUNKS[0] // 2, CHUNKS[0] // 2)
+            send_x(n, 0, tp.at[0, at, own], relay.at[at], device)
 
     def terms(i, c):
-        at = pl.ds(c * half, half)
+        at = chunk(c)
         base = targets[i] * wide
 
         @pl.loop(0, wide // 256, unroll=UT)
@@ -240,7 +263,7 @@
 
     def add_chip(i, c):
         t_copies[i, c].wait_recv()
-        add_rows(i, c * half, half)
+        add_rows(i, starts[c], CHUNKS[c])
 
     def add_rows(i, base, size):
         @pl.loop(0, size // step_rows, unroll=True)
@@ -249,11 +272,11 @@
             tp[i, at, own] = (tp[i, at, own].astype(F32) + trecv[i, at, :].astype(F32)).astype(BF16)
 
     def add_relay(i, rel, c, base):
-        @pl.loop(0, quarter // step_rows, unroll=True)
+        @pl.loop(0, CHUNKS[c] // 2 // step_rows, unroll=True)
         def _(r):
             off = pl.multiple_of(r * step_rows, step_rows)
             at = pl.ds(base + off, step_rows)
-            tp[i, at, own] = (tp[i, at, own].astype(F32) + rel[c, pl.ds(off, step_rows), :].astype(F32)).astype(BF16)
+            tp[i, at, own] = (tp[i, at, own].astype(F32) + rel[pl.ds(base + off, step_rows), :].astype(F32)).astype(BF16)
 
     def send_x(n, c, src, dst, device):
         x_copies[n, c] = send(src, dst, x_s, x_r, 6 * c + n, device)
@@ -261,8 +284,8 @@
     def far_out(c):
         qa, qb = quarters(c)
         add_chip(0, c)
-        send_x(0, c, tp.at[0, qa, own], relay_p.at[c], right)
-        send_x(1, c, tp.at[0, qb, own], relay_m.at[c], left)
+        send_x(0, c, tp.at[0, qa, own], relay_p.at[qa], right)
+        send_x(1, c, tp.at[0, qb, own], relay_m.at[qb], left)
 
     def right_out(c):
         qa, qb = quarters(c)
@@ -277,10 +300,10 @@
     def relayed(c):
         qa, qb = quarters(c)
         x_copies[0, c].wait_recv()
-        add_relay(1, relay_p, c, 2 * c * quarter)
+        add_relay(1, relay_p, c, starts[c])
         send_x(4, c, tp.at[1, qa, own], fin_p.at[qa], right)
         x_copies[1, c].wait_recv()
-        add_relay(2, relay_m, c, (2 * c + 1) * quarter)
+        add_relay(2, relay_m, c, starts[c] + CHUNKS[c] // 2)
         send_x(5, c, tp.at[2, qb, own], fin_m.at[qb], left)
 
     def to_other(n, c, block, at):
@@ -304,9 +327,9 @@
         for n in (2, 3, 4, 5):
             x_copies[n, c].wait_recv()
 
-        @pl.loop(0, half // step_rows, unroll=True)
+        @pl.loop(0, CHUNKS[c] // step_rows, unroll=True)
         def _(r):
-            at = pl.ds(pl.multiple_of(c * half + r * step_rows, step_rows), step_rows)
+            at = pl.ds(pl.multiple_of(starts[c] + r * step_rows, step_rows), step_rows)
             pred = tp[3, at, own].astype(F32) + trecv[3, at, :].astype(F32)
             pred = pred + fin_p[at, :].astype(F32) + fin_m[at, :].astype(F32)
             miss = pred - teacher[at, :].astype(F32)
@@ -317,7 +340,7 @@
         to_x(1, c, x, qb, left)
         to_x(2, c, x, qb, right)
         to_x(3, c, x, qa, left)
-        to_other(0, c, x, pl.ds(c * half, half))
+        to_other(0, c, x, chunk(c))
 
     def near_first(c):
         qa, qb = quarters(c)
@@ -343,7 +366,7 @@
         to_other(6, c, far, qb)
 
     def contract(block, c, lo=0, size=wide, fresh=False):
-        at = pl.ds(c * half, half)
+        at = chunk(c)
 
         @pl.loop(0, heads * DH // 256, unroll=UC)
         def _(n):
@@ -356,7 +379,7 @@
             acc[at, cols] = new if fresh else acc[at, cols] + new
 
     def contract_own(c):
-        from_other(0, c, x, pl.ds(c * half, half))
+        from_other(0, c, x, chunk(c))
         contract(x, c, fresh=True)
 
     def contract_near(c):
@@ -381,7 +404,7 @@
     right_out(0)
     terms(3, 0)
     left_out(0)
-    attend(half, half)
+    attend(starts[1], CHUNKS[1])
     terms(0, 1)
     relayed(0)
     terms(1, 1)
@@ -405,9 +428,9 @@
     @pl.loop(0, heads, unroll=True)
     def _(h):
         cols = lanes(h * DH, DH)
-        g_h = acc[0:half, cols].astype(BF16)
-        g[0:half, cols] = g_h
-        acc[0:DH, cols] = dot(q[0:half, cols], g_h, TN)
+        g_h = acc[0:CHUNKS[0], cols].astype(BF16)
+        g[0:CHUNKS[0], cols] = g_h
+        acc[0:DH, cols] = dot(q[0:CHUNKS[0], cols], g_h, TN)
 
     near_first(1)
     near_second(1)
@@ -418,9 +441,9 @@
     @pl.loop(0, heads, unroll=True)
     def _(h):
         cols = lanes(h * DH, DH)
-        g_h = acc[half:rows, cols].astype(BF16)
-        g[half:rows, cols] = g_h
-        loc2[head_rows(h), :] = (acc[0:DH, cols] + dot(q[half:rows, cols], g_h, TN)).astype(BF16)
+        g_h = acc[CHUNKS[0]:rows, cols].astype(BF16)
+        g[CHUNKS[0]:rows, cols] = g_h
+        loc2[head_rows(h), :] = (acc[0:DH, cols] + dot(q[CHUNKS[0]:rows, cols], g_h, TN)).astype(BF16)
 
     c_send = peers(True, loc2, got2, c_s, c_r, pr)
     start(c_send)
@@ -442,19 +465,15 @@
             dv[half:rows, cols] = dot(tri(k1, q1, upper), g1, NN)
 
     block_gradients(0, heads // 2)
-    finish_recv(peers(False, loc2, got2, c_s, c_r, pr))
-    scan(got2, pre2, True)
-    d_send = peers(True, pre2, state2, d_s, d_r, pr)
-    start(d_send)
-    state2[mine(pr), :] = pre2[mine(pr), :]
+    scan(loc2, got2, pre2, state2, c_s, c_r, d_s, d_r, True)
     block_gradients(heads // 2, heads)
-    finish_send(b_send)
+    finish_scan(pre, state, b_s, b_r)
     finish_send(n_send)
     finish_send(sent)
     finish_send(c_send)
     finish_recv(peers(False, pre2, state2, d_s, d_r, pr))
     suffix[...] = state2[...]
-    finish_send(d_send)
+    finish_scan(pre2, state2, d_s, d_r)
 
 
 def gradients(scale, k, v, dq, pk, pv, suffix, dq_out, dk_out, dv_out, dk, dv, sems):
@@ -483,7 +502,6 @@
     model = out_weight.shape[1]
     n_ctx = lax.axis_size("ctx")
     n_x = lax.axis_size("head") // 2
-    half = rows // 2
     wide = model // n_x
     part = wide // 2
     tokens = float(rows * n_ctx)
@@ -508,8 +526,8 @@
             pltpu.VMEM((rows, width), BF16),
             pltpu.VMEM((4, rows, wide), BF16),
             pltpu.VMEM((4, rows, part), BF16),
-            pltpu.VMEM((2, half // 2, part), BF16),
-            pltpu.VMEM((2, half // 2, part), BF16),
+            pltpu.VMEM((rows, part), BF16),
+            pltpu.VMEM((rows, part), BF16),
             pltpu.VMEM((rows, part), BF16),
             pltpu.VMEM((rows, part), BF16),
             pltpu.VMEM((n_x, rows, wide), BF16),

time: 86 us -> 86.1 us (level)
  no operation moved by 1% of the time
where the time goes in v6:
time: 86.1 us; the launch traced here: 85.6 us
  Pallas kernels  84.8 us (98%)
    pallas_call x1, Pallas kernels, on_device(): pl.pallas_call(functools.partial(transfer, scale, heads, n_ctx, n_x, toke...  82.1 us
    pallas_call x1, Pallas kernels, on_device(): pl.pallas_call(functools.partial(gradients, scale), name='gradients', out...  2.73 us

profile of v6, /device:TPU:1, one launch (start us, length us, event | category | flops | bytes accessed | tf_op | source)
XLA Modules:
  0.0 85.6 jit_solution(6749614411804662792)
XLA Ops:
  0.6 82.1 %transfer.1 = (bf16[512,1024]{1,0:T(8,128)(2,1)S(1)}, bf16[512,1024]{1,0:T(8,128)(2,1)S(1)}, f32[512,1024]{1,0:T(8,128)S(1)}, f32[512,1024]{1,0:T(8,128)S(1)}, f...) custom-call(bf16[512,1024]{1,0:T(8,128)(2,1)} %q_hbm.1, bf16[512,1024]{1,0:T(8,128)(2,1)} %k_hbm.1, ...), custom_call_target="tpu_custom_call" | custom-call | tf_op jit(solution)/shard_map/transfer/pallas_call | solution.py:515
  82.7 2.7 %gradients.1 = (f32[512,1024]{1,0:T(8,128)}, f32[512,1024]{1,0:T(8,128)}, f32[512,1024]{1,0:T(8,128)}) custom-call(bf16[512,1024]{1,0:T(8,128)(2,1)S(1)} %get-tuple-element.9.k, bf16[512,1024]{1,0:T(8,128)(2,1)S(1)} %get-tuple-element.10.v, f32[512,1024]{1,0:T(8,128)S(1)} %get-tuple-element.11.dq, f32[512,1024]{1,0:T(8,128)S(1)} %get-tuple-element.12.pk, ...), custom_call_target="tpu_custom_call" | custom-call | tf_op jit(solution)/shard_map/gradients/pallas_call | solution.py:552
